TPU v7x, 512 devices: a whole 4x4x16 slice. The times are simulated.
512 devices in a mesh: fy: 32 (over y, x, core), fx: 16 (over z).
Axes of the slice: x: 4, y: 4, z: 16, core: 2. Of those that a mesh axis runs over, the one named last changes fastest.
Arguments:
- start_image: float32 [16, 1024, 2048], P(None, 'fy', 'fx'), may hold values from 0.2 to 2
- dirty: float32 [16, 1024, 2048], P(None, 'fy', 'fx'), may hold values from -50 to 50
- sampling: float32 [16, 1024, 2048], P(None, 'fy', 'fx'), may hold values from 0.25 to 1
- basis_seed: float32 [16, 4], replicated, may hold values from -0.75 to 2.75
- margin: int32 [32, 16, 2, 2], P('fy', 'fx'), may hold values from 8 to 30, as said below
Outputs:
- image: float32 [16, 1024, 2048], P(None, 'fy', 'fx')
- data_dual: float32 [16, 1024, 2048], P(None, 'fy', 'fx')
Inputs may be any that keep to these rules, and one draw needn't show every extreme that they name: margin[a, b, l, 0] and margin[a, b, l, 1] are the widths kept above and to the left at dilation 2^l, at most 15 * 2^l; the value 30 occurs at the widest dilation in every draw.
All inputs are finite; a program needn't handle non-finite values.
Results may differ from a plain program's by a relative error of at most 0.0003.
Values sent between devices are 32-bit elements; how exact they have to be, the bound alone decides.
A program may use at most 64 MiB of HBM per device.

v0:
```python
import math

import jax
import jax.numpy as jnp
from jax import lax
from jax.sharding import Mesh
from jax.sharding import PartitionSpec as P

LEVELS = 2
REACH = 30
FY = ("fy_0", "fy_1", "fy_2")


DAUBECHIES = [
    -0.00011747678400228192,
    0.0006754494059985568,
    -0.0003917403729959771,
    -0.00487035299301066,
    0.008746094047015655,
    0.013981027917015516,
    -0.04408825393106472,
    -0.01736930100202211,
    0.128747426620186,
    0.00047248457399797254,
    -0.2840155429624281,
    -0.015829105256023893,
    0.5853546836548691,
    0.6756307362980128,
    0.3128715909144659,
    0.05441584224308161,
]
DUAL_STEP = 0.5
PRIMAL_STEP = 0.5
CLIP_LEVEL = 0.08
BALL_SCALE = 0.8
NORM_EPS = 1e-06


def passed_along(value, axis, steps):
    count = lax.axis_size(axis)
    first, last = (max(0, -steps), min(count, count - steps))
    return lax.ppermute(value, axis, [(source, source + steps) for source in range(first, last)])


def from_everyone(value, axis):
    length = lax.axis_size(axis)
    return lax.all_to_all(
        jnp.broadcast_to(value[None], (length, *value.shape)), axis, 0, 0, tiled=True
    )


def over_copies(value, axis):
    everything = from_everyone(value, axis)
    return jnp.sum(everything, axis=0)


def one_axis_at_a_time(value, axes):
    far, near = axes
    return over_copies(over_copies(value, near), far)


def band_matrix(filter_taps, extent, border, dilation):
    rows_idx = jnp.arange(extent + border)[:, None]
    cols_idx = jnp.arange(extent)[None, :]
    offset = cols_idx + border - rows_idx
    matrix = jnp.zeros((extent + border, extent), jnp.float32)
    for tap_idx in range(len(filter_taps)):
        matrix = matrix + filter_taps[tap_idx] * (offset == tap_idx * dilation).astype(jnp.float32)
    return matrix


def level_tables(row_count, col_count, border, dilation):
    low_taps = [tap_value / math.sqrt(2.0) for tap_value in DAUBECHIES]
    high_taps = [
        (-1.0) ** tap_idx * low_taps[len(low_taps) - 1 - tap_idx]
        for tap_idx in range(len(low_taps))
    ]
    return (
        band_matrix(low_taps, row_count, border, dilation),
        band_matrix(high_taps, row_count, border, dilation),
        band_matrix(low_taps, col_count, border, dilation),
        band_matrix(high_taps, col_count, border, dilation),
    )


def facet_mask(widths_pair, row_count, col_count, border):
    row_keep = (jnp.arange(row_count + border) >= border - widths_pair[0]).astype(jnp.float32)
    col_keep = (jnp.arange(col_count + border) >= border - widths_pair[1]).astype(jnp.float32)
    return row_keep[:, None] * col_keep[None, :]


def analyse(extended, tables):
    low_rows, high_rows, low_cols, high_cols = tables
    highest = lax.Precision.HIGHEST
    col_low = jnp.einsum("cjv,vw->cjw", extended, low_cols, precision=highest)
    col_high = jnp.einsum("cjv,vw->cjw", extended, high_cols, precision=highest)
    band_lh = jnp.einsum("ji,cjw->ciw", low_rows, col_high, precision=highest)
    band_hl = jnp.einsum("ji,cjw->ciw", high_rows, col_low, precision=highest)
    band_hh = jnp.einsum("ji,cjw->ciw", high_rows, col_high, precision=highest)
    return jnp.stack([band_lh, band_hl, band_hh])


def synthesise(bands, tables):
    low_rows, high_rows, low_cols, high_cols = tables
    highest = lax.Precision.HIGHEST
    rows_high = jnp.einsum("ji,ciw->cjw", low_rows, bands[0], precision=highest) + jnp.einsum(
        "ji,ciw->cjw", high_rows, bands[2], precision=highest
    )
    rows_low = jnp.einsum("ji,ciw->cjw", high_rows, bands[1], precision=highest)
    return jnp.einsum("cjw,vw->cjv", rows_high, high_cols, precision=highest) + jnp.einsum(
        "cjw,vw->cjv", rows_low, low_cols, precision=highest
    )


def orthonormal(basis_seed):
    columns = []
    for column_idx in range(basis_seed.shape[1]):
        vector = basis_seed[:, column_idx]
        for previous in columns:
            vector = vector - jnp.sum(previous * vector) * previous
        vector = vector / jnp.sqrt(jnp.sum(vector * vector))
        columns.append(vector)
    return jnp.stack(columns, axis=1)


def project(spectral, stepped):
    highest = lax.Precision.HIGHEST
    weights = jnp.einsum("cr,cij->rij", spectral, stepped, precision=highest)
    return jnp.einsum("cr,rij->cij", spectral, weights, precision=highest)


def extend_local(tile, border):
    from_above = passed_along(tile[:, -border:, :], FY, 1)
    taller = jnp.concatenate([from_above, tile], axis=1)
    from_left = passed_along(taller[:, :, -border:], "fx", 1)
    return jnp.concatenate([from_left, taller], axis=2)


def retract_local(grown, border):
    arrived = passed_along(grown[:, :, :border], "fx", -1)
    interior = grown[:, :, border:]
    interior = jnp.concatenate(
        [interior[:, :, :-border], interior[:, :, -border:] + arrived], axis=2
    )
    arrived = passed_along(interior[:, :border, :], FY, -1)
    interior = interior[:, border:, :]
    return jnp.concatenate([interior[:, :-border, :], interior[:, -border:, :] + arrived], axis=1)


def per_device(start_image, dirty, sampling, basis_seed, margin):
    channels, row_count, col_count = start_image.shape
    widths = margin[0, 0]
    spectral = orthonormal(basis_seed)
    radius = BALL_SCALE * math.sqrt(
        channels * row_count * col_count * lax.axis_size(FY) * lax.axis_size("fx")
    )
    weight = 1.0 / math.sqrt(LEVELS)
    band_duals = [
        jnp.zeros((3, channels, row_count, col_count), jnp.float32) for level_idx in range(LEVELS)
    ]
    shifted = DUAL_STEP * sampling * start_image - DUAL_STEP * dirty
    energy = one_axis_at_a_time(jnp.sum(shifted * shifted), (("fy_0", "fy_1"), ("fy_2", "fx")))
    factor = jnp.maximum(0.0, 1.0 - DUAL_STEP * radius / jnp.sqrt(energy + NORM_EPS))
    data_dual = factor * shifted
    extended = extend_local(start_image, REACH)
    returned = jnp.zeros_like(extended)
    for level_idx in range(LEVELS):
        tables = level_tables(row_count, col_count, REACH, 2**level_idx)
        keep_mask = facet_mask(widths[level_idx], row_count, col_count, REACH)
        coefficients = analyse(extended * keep_mask, tables)
        band_duals[level_idx] = jnp.clip(DUAL_STEP * weight * coefficients, -CLIP_LEVEL, CLIP_LEVEL)
        returned = returned + synthesise(band_duals[level_idx], tables) * keep_mask
    prior_term = retract_local(returned, REACH)
    stepped = start_image - PRIMAL_STEP * (sampling * data_dual + weight * prior_term)
    updated = jnp.maximum(project(spectral, stepped), 0.0)
    return (updated, data_dual)


def solution(mesh):
    finer = Mesh(mesh.devices.reshape(4, 4, 2, mesh.shape["fx"]), ("fy_0", "fy_1", "fy_2", "fx"))
    placed = (P(None, FY, "fx"), P(None, FY, "fx"), P(None, FY, "fx"), P(), P(FY, "fx", None, None))
    return jax.shard_map(
        per_device,
        mesh=finer,
        in_specs=placed,
        out_specs=(P(None, FY, "fx"), P(None, FY, "fx")),
        check_vma=False,
    )
```

profile of v0, /device:TPU:1, one launch (start us, length us, event | category | flops | bytes accessed | tf_op | source)
XLA Modules:
  0.0 108.0 jit_solution(14171621680619529062)
XLA Ops:
  0.6 1.8 %multiply_reduce_fusion = f32[]{:T(128)} fusion(f32[16,32,128]{2,1,0:T(8,128)} %param.6, f32[16,32,128]{2,1,0:T(8,128)} %param.5, f32[16,32,128]{2,1,0:T(8,128)} %param.7), kind=kLoop, calls=%fused_computation.59 | loop fusion | flops 393215 | bytes 786436 | tf_op jit(solution)/shard_map/reduce_sum | solution.py:162
  2.5 1.3 %broadcast_in_dim.4 = f32[32,1,1]{2,1,0:T(1,128)} broadcast(f32[]{:T(128)} %multiply_reduce_fusion), dimensions={} | broadcast | bytes 132 | tf_op jit(solution)/shard_map/broadcast_in_dim | solution.py:48
  3.7 16.7 %all-to-all-start = ((f32[32,1,1]{2,1,0:T(1,128)}), f32[32,1,1]{2,1,0:T(1,128)S(1)}, u32[]{:S(2)}, u32[]{:S(2)}) async-start(f32[32,1,1]{2,1,0:T(1,128)} %broadcast_in_dim.4), calls=%async_computation | async-start | bytes 32768 | tf_op jit(solution)/shard_map/all_to_all | solution.py:47
  20.5 3.2 %collective-permute-start = (f32[16,30,128]{2,1,0:T(8,128)S(1)}, f32[16,30,128]{2,1,0:T(8,128)S(1)}, u32[]{:S(2)}, u32[]{:S(2)}) collective-permute-start(f32[16,30,128]{2,1,0:T(8,128)S(1)} %slice.88), channel_id=1, source_target_pairs={{0,16},{16,32},{32,48},{48,64},{64,80},{80,96},{96,112},{112,128},... | collective-permute-start | bytes 737288 | tf_op jit(solution)/shard_map/ppermute | solution.py:42
  25.8 1.3 %fusion.447 = (f32[]{:T(128)}, f32[]{:T(128)}, f32[]{:T(128)}) fusion(f32[16,1]{0,1:T(1,128)S(1)} %get-tuple-element.23, f32[16,4]{0,1:T(4,128)S(1)} %copy-done.3, f32[]{:T(128)} %get-tuple-element.22), kind=kLoop, calls=%fused_computation.482 | loop fusion | flops 125 | bytes 272 | tf_op jit(solution)/shard_map/reduce_sum | solution.py:120
  31.0 2.0 %multiply_reduce_fusion.5 = (f32[]{:T(128)}, f32[16]{0:T(128)S(1)}, f32[16]{0:T(128)S(1)}) fusion(f32[16,1]{0,1:T(1,128)S(1)} %get-tuple-element.23, f32[]{:T(128)} %get-tuple-element.10, f32[16,4]{0,1:T(4,128)S(1)} %copy-done.3, f32[]{:T(128)S(6)} %sqrt.16, f32[]{:T(128)} %get-tuple-element.22), kind=kLoop, calls=%fused_computation.502 | loop fusion | flops 111 | bytes 336 | tf_op jit(solution)/shard_map/reduce_sum | solution.py:120
  33.0 1.8 %multiply_reduce_fusion.3 = (f32[]{:T(128)}, f32[]{:T(128)}, f32[16]{0:T(128)S(1)}) fusion(f32[16]{0:T(128)S(1)} %get-tuple-element.21, f32[16]{0:T(128)S(1)} %get-tuple-element.20, f32[]{:T(128)} %get-tuple-element.19, f32[16,1]{0,1:T(1,128)S(1)} %get-tuple-element.23, f32[]{:T(128)} %get-tuple-element.8, f32[16,4]{0,1:T(4,128)S(1)} %copy-done.3), kind=kLoop, calls=%fused_computation.498 | loop fusion | flops 126 | bytes 336 | tf_op jit(solution)/shard_map/reduce_sum | solution.py:120
  35.1 3.4 %collective-permute-start.1 = (f32[16,62,30]{2,1,0:T(8,128)S(1)}, f32[16,62,30]{2,1,0:T(8,128)S(1)}, u32[]{:S(2)}, u32[]{:S(2)}) collective-permute-start(f32[16,62,30]{2,1,0:T(8,128)S(1)} %pad_maximum_fusion), channel_id=1, source_target_pairs={{0,1},{1,2},{2,3},{3,4},{4,5},{5,6},{6,7},{7,8},{8,9},{9,10},{10,1... | collective-permute-start | bytes 357128 | tf_op jit(solution)/shard_map/ppermute | solution.py:42
  39.3 10.5 %collective-permute-done.1 = f32[16,62,30]{2,1,0:T(8,128)S(1)} collective-permute-done((f32[16,62,30]{2,1,0:T(8,128)S(1)}, f32[16,62,30]{2,1,0:T(8,128)S(1)}, u32[]{:S(2)}, u32[]{:S(2)}) %collective-permute-start.1) | collective-permute-done | bytes 119072 | tf_op jit(solution)/shard_map/ppermute | solution.py:42
  49.7 1.2 %fusion.7 = f32[16,62,128]{2,1,0:T(8,128)S(1)} fusion(f32[62,158]{1,0:T(8,128)S(1)} %broadcast_multiply_fusion.1, f32[16,32,128]{2,1,0:T(8,128)S(1)} %copy-done, f32[16,30,128]{2,1,0:T(8,128)S(1)} %collective-permute-done, f32[16,62,30]{2,1,0:T(8,128)S(1)} %collective-permute-done.1, s32[128]{0:T(128)S(1)} %iota_add_fusion.1), kind=kOutput, calls=%fused_computation.21 | convolution fusion | flops 242187456 | bytes 1174544 | tf_op jit(solution)/shard_map/cjv,vw->cjw/dot_general | solution.py:96
  51.9 1.2 %fusion.11 = f32[16,62,128]{2,1,0:T(8,128)S(1)} fusion(f32[62,158]{1,0:T(8,128)S(1)} %broadcast_multiply_fusion.2, f32[16,32,128]{2,1,0:T(8,128)S(1)} %copy-done, f32[16,30,128]{2,1,0:T(8,128)S(1)} %collective-permute-done, f32[16,62,30]{2,1,0:T(8,128)S(1)} %collective-permute-done.1, s32[128]{0:T(128)S(1)} %iota_add_fusion.1), kind=kOutput, calls=%fused_computation.25 | convolution fusion | flops 242187456 | bytes 1174544 | tf_op jit(solution)/shard_map/cjv,vw->cjw/dot_general | solution.py:96
  54.1 1.2 %fusion.9 = f32[16,62,128]{2,1,0:T(8,128)S(1)} fusion(f32[62,158]{1,0:T(8,128)S(1)} %broadcast_multiply_fusion.2, f32[16,32,128]{2,1,0:T(8,128)S(1)} %copy-done, f32[16,30,128]{2,1,0:T(8,128)S(1)} %collective-permute-done, f32[16,62,30]{2,1,0:T(8,128)S(1)} %collective-permute-done.1, s32[128]{0:T(128)S(1)} %iota_add_fusion.1), kind=kOutput, calls=%fused_computation.23 | convolution fusion | flops 242187456 | bytes 1174544 | tf_op jit(solution)/shard_map/cjv,vw->cjw/dot_general | solution.py:95
  57.3 1.2 %fusion.5 = f32[16,62,128]{2,1,0:T(8,128)S(1)} fusion(f32[62,158]{1,0:T(8,128)S(1)} %broadcast_multiply_fusion.1, f32[16,32,128]{2,1,0:T(8,128)S(1)} %copy-done, f32[16,30,128]{2,1,0:T(8,128)S(1)} %collective-permute-done, f32[16,62,30]{2,1,0:T(8,128)S(1)} %collective-permute-done.1, s32[128]{0:T(128)S(1)} %iota_add_fusion.1), kind=kOutput, calls=%fused_computation.19 | convolution fusion | flops 242187456 | bytes 1174544 | tf_op jit(solution)/shard_map/cjv,vw->cjw/dot_general | solution.py:95
  64.4 1.1 %fusion.2 = f32[16,62,158]{2,1,0:T(8,128)S(1)} fusion(f32[16,62,158]{2,1,0:T(8,128)S(1)} %fusion.87, f32[16,62,128]{2,1,0:T(8,128)S(1)} %convolution_bitcast_fusion.1, f32[62,158]{1,0:T(8,128)S(1)} %broadcast_multiply_fusion.2, s32[128]{0:T(128)S(1)} %iota_add_fusion.1), kind=kOutput, calls=%fused_computation.4 | convolution fusion | flops 242030720 | bytes 1801488 | tf_op jit(solution)/shard_map/cjw,vw->cjv/dot_general | solution.py:110
  65.5 1.1 %fusion.1 = f32[16,62,158]{2,1,0:T(8,128)S(1)} fusion(f32[16,62,158]{2,1,0:T(8,128)S(1)} %fusion.2, f32[16,62,158]{2,1,0:T(8,128)S(1)} %fusion.126, f32[16,62,128]{2,1,0:T(8,128)S(1)} %convolution_bitcast_fusion, f32[62,158]{1,0:T(8,128)S(1)} %broadcast_multiply_fusion.1, s32[128]{0:T(128)S(1)} %iota_add_fusion.1), kind=kOutput, calls=%fused_computation.2 | convolution fusion | flops 242187456 | bytes 2428432 | tf_op jit(solution)/shard_map/cjw,vw->cjv/dot_general | solution.py:110
  66.6 1.3 %collective-permute-start.2 = (f32[16,62,30]{2,1,0:T(8,128)S(1)}, f32[16,62,30]{2,1,0:T(8,128)S(1)}, u32[]{:S(2)}, u32[]{:S(2)}) collective-permute-start(f32[16,62,30]{2,1,0:T(8,128)S(1)} %slice.114), channel_id=1, source_target_pairs={{1,0},{2,1},{3,2},{4,3},{5,4},{6,5},{7,6},{8,7},{9,8},{10,9},{11,1... | collective-permute-start | bytes 357128 | tf_op jit(solution)/shard_map/ppermute | solution.py:42
  67.9 1.9 %multiply_reduce_fusion.2 = (f32[]{:T(128)}, f32[16]{0:T(128)S(1)}) fusion(f32[16]{0:T(128)S(1)} %get-tuple-element.18, f32[16]{0:T(128)S(1)} %get-tuple-element.21, f32[]{:T(128)} %get-tuple-element.11, f32[]{:T(128)S(6)} %sqrt.17, f32[16]{0:T(128)S(1)} %get-tuple-element.20, f32[]{:T(128)} %get-tuple-element.19), kind=kLoop, calls=%fused_computation.496 | loop fusion | flops 111 | bytes 272 | tf_op jit(solution)/shard_map/reduce_sum | solution.py:120
  70.0 12.5 %collective-permute-done.2 = f32[16,62,30]{2,1,0:T(8,128)S(1)} collective-permute-done((f32[16,62,30]{2,1,0:T(8,128)S(1)}, f32[16,62,30]{2,1,0:T(8,128)S(1)}, u32[]{:S(2)}, u32[]{:S(2)}) %collective-permute-start.2) | collective-permute-done | bytes 119072 | tf_op jit(solution)/shard_map/ppermute | solution.py:42
  82.8 2.7 %collective-permute-start.3 = (f32[16,30,128]{2,1,0:T(8,128)S(1)}, f32[16,30,128]{2,1,0:T(8,128)S(1)}, u32[]{:S(2)}, u32[]{:S(2)}) collective-permute-start(f32[16,30,128]{2,1,0:T(8,128)S(1)} %pad_maximum_fusion.1), channel_id=1, source_target_pairs={{16,0},{32,16},{48,32},{64,48},{80,64},{96,80},{112,96},{128,112},... | collective-permute-start | bytes 737288 | tf_op jit(solution)/shard_map/ppermute | solution.py:42
  85.5 1.9 %multiply_reduce_fusion.1 = f32[]{:T(128)} fusion(f32[16]{0:T(128)S(1)} %get-tuple-element.17, f32[]{:T(128)} %get-tuple-element.16, f32[16]{0:T(128)S(1)} %get-tuple-element.18, f32[16]{0:T(128)S(1)} %get-tuple-element.21, f32[]{:T(128)} %get-tuple-element.11), kind=kLoop, calls=%fused_computation.494 | loop fusion | flops 95 | bytes 204 | tf_op jit(solution)/shard_map/reduce_sum | solution.py:121
  88.7 1.2 %broadcast_in_dim.5 = f32[16,1,1]{2,1,0:T(1,128)} broadcast(f32[]{:T(128)} %reduce_sum.128), dimensions={} | broadcast | bytes 68 | tf_op jit(solution)/shard_map/broadcast_in_dim | solution.py:48
  89.9 6.8 %all-to-all-start.1 = ((f32[16,1,1]{2,1,0:T(1,128)}), f32[16,1,1]{2,1,0:T(1,128)S(1)}, u32[]{:S(2)}, u32[]{:S(2)}) async-start(f32[16,1,1]{2,1,0:T(1,128)} %broadcast_in_dim.5), calls=%async_computation.1 | async-start | bytes 16384 | tf_op jit(solution)/shard_map/all_to_all | solution.py:47
  96.7 3.7 %subtract_divide_fusion = (f32[16,1]{0,1:T(1,128)S(1)}, f32[16,1]{0,1:T(1,128)S(1)}, f32[16,1]{0,1:T(1,128)S(1)}) fusion(f32[16,1]{0,1:T(1,128)S(1)} %get-tuple-element.23, f32[]{:T(128)S(6)} %sqrt.18, f32[]{:T(128)} %get-tuple-element.16, f32[]{:T(128)} %get-tuple-element.11, f32[]{:T(128)} %get-tuple-element.8, f32[16,4]{0,1:T(4,128)S(1)} %copy-done.3, ...), kind=kLoop, calls=%fused_computation.495 | loop fusion | flops 240 | bytes 484 | tf_op jit(solution)/shard_map/div | solution.py:121
  100.5 2.6 %all-to-all-done.1 = f32[16,1,1]{2,1,0:T(1,128)S(1)} async-done(((f32[16,1,1]{2,1,0:T(1,128)}), f32[16,1,1]{2,1,0:T(1,128)S(1)}, u32[]{:S(2)}, u32[]{:S(2)}) %all-to-all-start.1) | async-done | bytes 96 | tf_op jit(solution)/shard_map/all_to_all | solution.py:47
  (53 shorter events, 17.4 us)
Async XLA Ops:
  0.6 19.9 %copy-start = (f32[16,32,128]{2,1,0:T(8,128)S(1)}, f32[16,32,128]{2,1,0:T(8,128)}, u32[]{:S(2)}) copy-start(f32[16,32,128]{2,1,0:T(8,128)} %param.5) | copy-start | bytes 786436
  3.7 84.3 %all-to-all-start = ((f32[32,1,1]{2,1,0:T(1,128)}), f32[32,1,1]{2,1,0:T(1,128)S(1)}, u32[]{:S(2)}, u32[]{:S(2)}) async-start(f32[32,1,1]{2,1,0:T(1,128)} %broadcast_in_dim.4), calls=%async_computation | async-start | bytes 32768 | tf_op jit(solution)/shard_map/all_to_all | solution.py:47
  20.5 3.3 %copy-start.3 = (f32[16,4]{0,1:T(4,128)S(1)}, f32[16,4]{0,1:T(4,128)}, u32[]{:S(2)}) copy-start(f32[16,4]{0,1:T(4,128)} %param.8) | copy-start | bytes 772
  20.5 14.3 %collective-permute-start = (f32[16,30,128]{2,1,0:T(8,128)S(1)}, f32[16,30,128]{2,1,0:T(8,128)S(1)}, u32[]{:S(2)}, u32[]{:S(2)}) collective-permute-start(f32[16,30,128]{2,1,0:T(8,128)S(1)} %slice.88), channel_id=1, source_target_pairs={{0,16},{16,32},{32,48},{48,64},{64,80},{80,96},{96,112},{112,128},... | collective-permute-start | bytes 737288 | tf_op jit(solution)/shard_map/ppermute | solution.py:42
  27.1 0.7 copy-start.4
  35.1 14.6 %collective-permute-start.1 = (f32[16,62,30]{2,1,0:T(8,128)S(1)}, f32[16,62,30]{2,1,0:T(8,128)S(1)}, u32[]{:S(2)}, u32[]{:S(2)}) collective-permute-start(f32[16,62,30]{2,1,0:T(8,128)S(1)} %pad_maximum_fusion), channel_id=1, source_target_pairs={{0,1},{1,2},{2,3},{3,4},{4,5},{5,6},{6,7},{7,8},{8,9},{9,10},{10,1... | collective-permute-start | bytes 357128 | tf_op jit(solution)/shard_map/ppermute | solution.py:42
  66.6 15.9 %collective-permute-start.2 = (f32[16,62,30]{2,1,0:T(8,128)S(1)}, f32[16,62,30]{2,1,0:T(8,128)S(1)}, u32[]{:S(2)}, u32[]{:S(2)}) collective-permute-start(f32[16,62,30]{2,1,0:T(8,128)S(1)} %slice.114), channel_id=1, source_target_pairs={{1,0},{2,1},{3,2},{4,3},{5,4},{6,5},{7,6},{8,7},{9,8},{10,9},{11,1... | collective-permute-start | bytes 357128 | tf_op jit(solution)/shard_map/ppermute | solution.py:42
  82.8 21.6 %collective-permute-start.3 = (f32[16,30,128]{2,1,0:T(8,128)S(1)}, f32[16,30,128]{2,1,0:T(8,128)S(1)}, u32[]{:S(2)}, u32[]{:S(2)}) collective-permute-start(f32[16,30,128]{2,1,0:T(8,128)S(1)} %pad_maximum_fusion.1), channel_id=1, source_target_pairs={{16,0},{32,16},{48,32},{64,48},{80,64},{96,80},{112,96},{128,112},... | collective-permute-start | bytes 737288 | tf_op jit(solution)/shard_map/ppermute | solution.py:42
  89.9 13.2 %all-to-all-start.1 = ((f32[16,1,1]{2,1,0:T(1,128)}), f32[16,1,1]{2,1,0:T(1,128)S(1)}, u32[]{:S(2)}, u32[]{:S(2)}) async-start(f32[16,1,1]{2,1,0:T(1,128)} %broadcast_in_dim.5), calls=%async_computation.1 | async-start | bytes 16384 | tf_op jit(solution)/shard_map/all_to_all | solution.py:47
  104.4 1.0 copy-start.1
  104.4 1.0 copy-start.2
where the time goes:
time: 110 us; the launch traced here: 108 us
  starting transfers between devices  34.2 us (31%)
  waiting for transfers between devices  25.6 us (23%)
  other arithmetic  18.7 us (17%)
  matrix products  17.4 us (16%)
  between operations  6.96 us (6%)
  local copies, waits for them, and re-layouts  5.08 us (5%)
    all_to_all x2, starting transfers between devices, from_everyone(): lax.all_to_all(jnp.broadcast_to(value[None], (length, *value.shape)), axi...  23.6 us
    ppermute x4, waiting for transfers between devices, passed_along(): lax.ppermute(value, axis, [(source, source + steps) for source in range(f...  23 us
    ppermute x4, starting transfers between devices, passed_along(): lax.ppermute(value, axis, [(source, source + steps) for source in range(f...  10.6 us
    reduce_sum x5, other arithmetic, orthonormal(): vector = vector - jnp.sum(previous * vector) * previous  7.64 us
    div x1, other arithmetic, orthonormal(): vector = vector / jnp.sqrt(jnp.sum(vector * vector))  3.75 us
    all_to_all x2, waiting for transfers between devices, from_everyone(): lax.all_to_all(jnp.broadcast_to(value[None], (length, *value.shape)), axi...  2.61 us
    broadcast_in_dim x2, local copies, waits for them, and re-layouts, from_everyone(): jnp.broadcast_to(value[None], (length, *value.shape))  2.51 us
    reduce_sum x2, other arithmetic, orthonormal(): vector = vector / jnp.sqrt(jnp.sum(vector * vector))  2.45 us
  transfers between devices with their start and end apart: 6, of which 3 were waited for; matrix products, arithmetic and copies ran while one was open for 32% of the time, Pallas kernels for 0%

commit v1 on v0

v1 whole, which is shorter than its diff:
```python
import math

import jax
import jax.numpy as jnp
import numpy as np
from jax import lax
from jax.experimental import pallas as pl
from jax.experimental.pallas import tpu as pltpu
from jax.sharding import PartitionSpec as P

MESH = pl.DeviceIdType.MESH
BF = jnp.bfloat16
F32 = jnp.float32

LEVELS = 2
PAD = 32
ROWS = 32
COLS = 128
CHANNELS = 16
RANK = 4
HALVES = 2
PER = CHANNELS // HALVES
GROUPS = CHANNELS // 4


DAUBECHIES = [
    -0.00011747678400228192,
    0.0006754494059985568,
    -0.0003917403729959771,
    -0.00487035299301066,
    0.008746094047015655,
    0.013981027917015516,
    -0.04408825393106472,
    -0.01736930100202211,
    0.128747426620186,
    0.00047248457399797254,
    -0.2840155429624281,
    -0.015829105256023893,
    0.5853546836548691,
    0.6756307362980128,
    0.3128715909144659,
    0.05441584224308161,
]
DUAL_STEP = 0.5
PRIMAL_STEP = 0.5
CLIP_LEVEL = 0.08
BALL_SCALE = 0.8
NORM_EPS = 1e-06


def taps_pair():
    low = [tap / math.sqrt(2.0) for tap in DAUBECHIES]
    high = [(-1.0) ** k * low[len(low) - 1 - k] for k in range(len(low))]
    return low, high


def band_matrix(taps, extent, dilation):
    matrix = np.zeros((extent + PAD, extent), np.float64)
    for k, tap in enumerate(taps):
        for i in range(extent):
            matrix[i + PAD - k * dilation, i] += tap
    return matrix


def split_host(matrix):
    high = matrix.astype(np.float32).astype(jnp.bfloat16)
    low = (matrix - high.astype(np.float64)).astype(np.float32).astype(jnp.bfloat16)
    return high, low


def tables():
    low, high = taps_pair()
    scale = DUAL_STEP / math.sqrt(LEVELS)
    rows, cols = [], []
    for level in range(LEVELS):
        d = 2**level
        rows.append(band_matrix(low, ROWS, d).T)
        rows.append(band_matrix(high, ROWS, d).T)
        both = np.concatenate([band_matrix(low, COLS, d), band_matrix(high, COLS, d)], axis=1) * scale
        cols.append(np.concatenate([both[PAD:]] + [both[:PAD]] * 4, axis=0))
    row_all = np.concatenate(rows, axis=0)
    hi, lo = (part.astype(np.float32) for part in split_host(row_all))
    forward = np.concatenate([hi, hi, lo], axis=1)
    backward = np.concatenate([hi.T, hi.T, lo.T], axis=1)
    column = []
    for level in range(LEVELS):
        column.extend(split_host(cols[level]))
    for level in range(LEVELS):
        column.extend(split_host(cols[level].T))
    return forward, backward, np.stack(column)


def split(value):
    high = value.astype(BF)
    return high, (value - high.astype(F32)).astype(BF)


def dot(a, b):
    return jnp.dot(a, b, preferred_element_type=F32)


def kernel_body(fy_count, fx_count, start_hbm, dirty_hbm, samp_hbm, basis_hbm, margin_hbm, fwd_hbm, bwd_hbm, col_hbm,
                pa_ref, pb_ref, shifted_ref, factor_ref,
                start, dirty, samp, basis, margin, fwd_raw, bwd_raw, col,
                fwd_m, bwd_m, pack, above, left_in, corner_in,
                x_own, x_left, lhs, bands, z_own, z_left, own, up_out, left_out, up_in, left_back, corner_back,
                spec, e_send, e_recv, f_send, f_recv,
                load_sem, halo_send, halo_recv, e_sem, f_sem, back_send, back_recv):
    me_y, me_x = lax.axis_index("fy"), lax.axis_index("fx")
    below, over = lax.rem(me_y + 1, fy_count), lax.rem(me_y + fy_count - 1, fy_count)
    right, left = lax.rem(me_x + 1, fx_count), lax.rem(me_x + fx_count - 1, fx_count)

    loads = []
    for at, (source, target) in enumerate([(start_hbm, start), (dirty_hbm, dirty), (samp_hbm, samp), (margin_hbm, margin),
                                           (basis_hbm, basis), (fwd_hbm, fwd_raw), (bwd_hbm, bwd_raw), (col_hbm, col)]):
        copy = pltpu.make_async_copy(source, target, load_sem.at[at])
        copy.start()
        loads.append(copy)

    barrier = pltpu.get_barrier_semaphore()

    def greet(device):
        pl.semaphore_signal(barrier, inc=1, device_id=device, device_id_type=MESH)

    def greet_x(k, carry):
        greet({"fy": me_y, "fx": lax.rem(me_x + k, fx_count)})
        return carry

    def greet_y(k, carry):
        greet({"fy": lax.rem(me_y + k, fy_count), "fx": me_x})
        return carry

    lax.fori_loop(1, fx_count, greet_x, 0)
    lax.fori_loop(1, fy_count, greet_y, 0)
    greet({"fy": below, "fx": right})
    greet({"fy": over, "fx": left})

    lane = lax.broadcasted_iota(jnp.int32, (1, COLS), 1)
    block = lane // PAD

    loads[0].wait()
    for g in range(GROUPS):
        total = jnp.zeros((ROWS, COLS), F32)
        for q in range(4):
            value = start[4 * g + q]
            moved = value if q == 3 else pltpu.roll(value, PAD * (q + 1), 1)
            total = jnp.where(block == q, moved, total)
        pack[g] = total
    loads[1].wait()
    loads[2].wait()
    energy = jnp.zeros((ROWS, COLS), F32)
    for c in range(CHANNELS):
        value = DUAL_STEP * samp[c] * start[c] - DUAL_STEP * dirty[c]
        shifted_ref[c] = value
        energy = energy + value * value
    energy = jnp.sum(energy, axis=0, keepdims=True)
    e_send[...] = energy
    e_recv[me_y] = energy

    pl.semaphore_wait(barrier, fx_count + fy_count)

    def energy_copy(k):
        return pltpu.make_async_remote_copy(
            src_ref=e_send, dst_ref=e_recv.at[me_y], send_sem=e_sem.at[0], recv_sem=e_sem.at[1],
            device_id={"fy": lax.rem(me_y + k, fy_count), "fx": me_x}, device_id_type=MESH)

    def energy_start(k, carry):
        energy_copy(k).start()
        return carry

    lax.fori_loop(1, fy_count, energy_start, 0)

    halos = []
    for h in range(HALVES):
        chans = pl.ds(h * PER, PER)
        groups = pl.ds(h * PER // 4, PER // 4)
        for at, (source, target, device) in enumerate([
            (start.at[chans], above.at[chans], {"fy": below, "fx": me_x}),
            (pack.at[groups], left_in.at[groups], {"fy": me_y, "fx": right}),
            (pack.at[groups], corner_in.at[groups], {"fy": below, "fx": right}),
        ]):
            copy = pltpu.make_async_remote_copy(
                src_ref=source, dst_ref=target, send_sem=halo_send.at[h, at], recv_sem=halo_recv.at[h, at],
                device_id=device, device_id_type=MESH)
            copy.start()
            halos.append(copy)

    for copy in loads[3:]:
        copy.wait()
    row_has = (me_y > 0).astype(jnp.int32)
    col_has = (me_x > 0).astype(jnp.int32)
    keep_rows = [margin[0, 0, l, 0] * row_has for l in range(LEVELS)]
    keep_cols = [margin[0, 0, l, 1] * col_has for l in range(LEVELS)]

    row_at = lax.broadcasted_iota(jnp.int32, (128, 192), 0)
    col_at = lax.rem(lax.broadcasted_iota(jnp.int32, (128, 192), 1), 64)
    reach = jnp.where(row_at < 64, keep_rows[0], keep_rows[1])
    fwd_m[...] = jnp.where(PAD - col_at <= reach, fwd_raw[...], 0.0).astype(BF)
    row_at = lax.broadcasted_iota(jnp.int32, (64, 384), 0)
    col_at = lax.rem(lax.broadcasted_iota(jnp.int32, (64, 384), 1), 128)
    reach = jnp.where(col_at < 64, keep_rows[0], keep_rows[1])
    bwd_m[...] = jnp.where(PAD - row_at <= reach, bwd_raw[...], 0.0).astype(BF)

    kept = []
    for l in range(LEVELS):
        inside = PAD - lax.rem(lane, PAD) <= keep_cols[l]
        kept.append([jnp.logical_and(inside, block == q) for q in range(4)])

    columns = []
    for r in range(RANK):
        vector = jnp.broadcast_to(basis[:, r : r + 1], (CHANNELS, COLS))
        for previous in columns:
            vector = vector - jnp.sum(previous * vector, axis=0, keepdims=True) * previous
        vector = vector / jnp.sqrt(jnp.sum(vector * vector, axis=0, keepdims=True))
        columns.append(vector)
        spec[r] = vector

    def project(field):
        weights = []
        for r in range(RANK):
            total = spec[r, 0:1, :] * field(0)
            for c in range(1, CHANNELS):
                total = total + spec[r, c : c + 1, :] * field(c)
            weights.append(total)

        def channel(c):
            total = spec[0, c : c + 1, :] * weights[0]
            for r in range(1, RANK):
                total = total + spec[r, c : c + 1, :] * weights[r]
            return total

        return channel

    pb = project(lambda c: PRIMAL_STEP * samp[c] * shifted_ref[c])
    for c in range(CHANNELS):
        pb_ref[c] = pb(c)

    def place(target, p, part, row0, value):
        high, low = split(value)
        lanes = pl.ds(COLS * part, COLS)
        target[p, pl.ds(row0, ROWS), lanes] = high
        target[p, pl.ds(64 + row0, ROWS), lanes] = low
        target[p, pl.ds(128 + row0, ROWS), lanes] = high

    for c in range(CHANNELS):
        place(x_own, c // 2, c % 2, PAD, start[c])

    pltpu.make_async_copy(e_recv.at[pl.ds(0, fy_count - 1)], e_recv.at[pl.ds(0, fy_count - 1)], e_sem.at[1]).wait()
    partial = jnp.sum(e_recv[...], axis=0)
    f_send[...] = partial
    f_recv[me_x] = partial

    def second_start(k, carry):
        pltpu.make_async_remote_copy(
            src_ref=f_send, dst_ref=f_recv.at[me_x], send_sem=f_sem.at[0], recv_sem=f_sem.at[1],
            device_id={"fy": me_y, "fx": lax.rem(me_x + k, fx_count)}, device_id_type=MESH).start()
        return carry

    lax.fori_loop(1, fx_count, second_start, 0)

    backs = []
    for h in range(HALVES):
        for copy in halos[3 * h : 3 * h + 3]:
            copy.wait_recv()
        first = h * PER
        for c in range(first, first + PER):
            place(x_own, c // 2, c % 2, 0, above[c])
        for g in range(first // 4, (first + PER) // 4):
            place(x_left, g // 2, g % 2, 0, corner_in[g])
            place(x_left, g // 2, g % 2, PAD, left_in[g])
        for p in range(first // 2, (first + PER) // 2):
            u = dot(fwd_m[...], x_own[p])
            high, low = split(u)
            for part in range(2):
                c = 2 * p + part - first
                lanes = slice(COLS * part, COLS * (part + 1))
                for l in range(LEVELS):
                    lhs[l, pl.ds(64 * c, 64), 0:128] = high[64 * l : 64 * l + 64, lanes]
                    lhs[l, pl.ds(64 * c, 64), 256:384] = low[64 * l : 64 * l + 64, lanes]
        for p in range(first // 8, (first + PER) // 8):
            u = dot(fwd_m[...], x_left[p])
            for part in range(2):
                for q in range(4):
                    c = 8 * p + 4 * part + q - first
                    for l in range(LEVELS):
                        value = jnp.where(kept[l][q], u[64 * l : 64 * l + 64, COLS * part : COLS * (part + 1)], 0.0)
                        high, low = split(value)
                        lhs[l, pl.ds(64 * c, 64), 128:256] = high
                        lhs[l, pl.ds(64 * c, 64), 384:512] = low
        z_sum = [[jnp.zeros((64, COLS), F32) for l in range(LEVELS)] for g in range(PER // 4)]
        for l in range(LEVELS):
            acc = dot(lhs[l, :, 0:256], col[2 * l]) + dot(lhs[l, :, 256:512], col[2 * l]) + dot(lhs[l, :, 0:256], col[2 * l + 1])
            acc = jnp.clip(acc, -CLIP_LEVEL, CLIP_LEVEL)
            high, low = split(acc)
            for c in range(PER):
                zero = jnp.zeros((32, COLS), BF)
                top, mid, end = 64 * c, 64 * c + 32, 64 * c + 64
                bands[pl.ds(top, 32), 0:128] = zero
                bands[pl.ds(top, 32), 256:384] = zero
                bands[pl.ds(top, 32), 128:256] = high[top:mid, 128:256]
                bands[pl.ds(top, 32), 384:512] = low[top:mid, 128:256]
                bands[pl.ds(mid, 32), 0:256] = high[mid:end, :]
                bands[pl.ds(mid, 32), 256:512] = low[mid:end, :]
            at = 2 * LEVELS + 2 * l
            z = dot(bands[:, 0:256], col[at]) + dot(bands[:, 256:512], col[at]) + dot(bands[:, 0:256], col[at + 1])
            for c in range(PER):
                high, low = split(z[64 * c : 64 * c + 64, 0:128])
                lanes = pl.ds(COLS * (c % 2), COLS)
                z_own[c // 2, pl.ds(64 * l, 64), lanes] = high
                z_own[c // 2, pl.ds(128 + 64 * l, 64), lanes] = low
                piece = z[64 * c : 64 * c + 64, 128:256]
                z_sum[c // 4][l] = z_sum[c // 4][l] + jnp.where(kept[l][c % 4], piece, 0.0)
        for g in range(PER // 4):
            lanes = pl.ds(COLS * (g % 2), COLS)
            for l in range(LEVELS):
                high, low = split(z_sum[g][l])
                z_left[g // 2, pl.ds(64 * l, 64), lanes] = high
                z_left[g // 2, pl.ds(128 + 64 * l, 64), lanes] = low
        for p in range(PER // 8):
            r = dot(bwd_m[:, 0:256], z_left[p]) + dot(bwd_m[:, 256:384], z_left[p, 0:128, :])
            for part in range(2):
                left_out[first // 4 + 2 * p + part] = r[:, COLS * part : COLS * (part + 1)]
        for p in range(PER // 2):
            r = dot(bwd_m[:, 0:256], z_own[p]) + dot(bwd_m[:, 256:384], z_own[p, 0:128, :])
            for part in range(2):
                c = first + 2 * p + part
                up_out[c] = r[0:32, COLS * part : COLS * (part + 1)]
                own[c] = r[32:64, COLS * part : COLS * (part + 1)]
        chans = pl.ds(first, PER)
        groups = pl.ds(first // 4, PER // 4)
        for at, (source, target, device) in enumerate([
            (left_out.at[groups, pl.ds(32, 32), :], left_back.at[groups], {"fy": me_y, "fx": left}),
            (left_out.at[groups, pl.ds(0, 32), :], corner_back.at[groups], {"fy": over, "fx": left}),
            (up_out.at[chans], up_in.at[chans], {"fy": over, "fx": me_x}),
        ]):
            copy = pltpu.make_async_remote_copy(
                src_ref=source, dst_ref=target, send_sem=back_send.at[h, at], recv_sem=back_recv.at[h, at],
                device_id=device, device_id_type=MESH)
            copy.start()
            backs.append(copy)

    for copy in backs:
        copy.wait_recv()
    for g in range(GROUPS):
        strip = left_back[g] + corner_back[g]
        for q in range(4):
            c = 4 * g + q
            moved = strip if q == 3 else pltpu.roll(strip, COLS - PAD * (q + 1), 1)
            own[c] = start[c] - (own[c] + up_in[c] + jnp.where(block == 3, moved, 0.0))
    pa = project(lambda c: own[c])
    for c in range(CHANNELS):
        pa_ref[c] = pa(c)

    pltpu.make_async_copy(f_recv.at[pl.ds(0, fx_count - 1)], f_recv.at[pl.ds(0, fx_count - 1)], f_sem.at[1]).wait()
    total = jnp.sum(jnp.sum(f_recv[...], axis=0), axis=1, keepdims=True)
    radius = BALL_SCALE * math.sqrt(CHANNELS * ROWS * COLS * fy_count * fx_count)
    factor = jnp.maximum(0.0, 1.0 - DUAL_STEP * radius / jnp.sqrt(total + NORM_EPS))
    factor_ref[...] = jnp.broadcast_to(factor, (1, COLS))

    for copy in halos + backs:
        copy.wait_send()
    pltpu.make_async_copy(e_recv.at[pl.ds(0, fy_count - 1)], e_recv.at[pl.ds(0, fy_count - 1)], e_sem.at[0]).wait()
    pltpu.make_async_copy(f_recv.at[pl.ds(0, fx_count - 1)], f_recv.at[pl.ds(0, fx_count - 1)], f_sem.at[0]).wait()


def per_device(fy_count, fx_count, start_image, dirty, sampling, basis_seed, margin):
    forward, backward, column = tables()
    tile = jax.ShapeDtypeStruct((CHANNELS, ROWS, COLS), F32)
    hbm = pl.BlockSpec(memory_space=pltpu.HBM)
    vmem = pl.BlockSpec(memory_space=pltpu.VMEM)
    field = pltpu.VMEM((CHANNELS, ROWS, COLS), F32)
    strips = pltpu.VMEM((GROUPS, ROWS, COLS), F32)
    dma = pltpu.SemaphoreType.DMA

    def body(*refs):
        kernel_body(fy_count, fx_count, *refs)

    pa, pb, shifted, factor = pl.pallas_call(
        body,
        out_shape=(tile, tile, tile, jax.ShapeDtypeStruct((1, COLS), F32)),
        in_specs=[hbm] * 8,
        out_specs=(vmem,) * 4,
        scratch_shapes=[
            field, field, field,
            pltpu.VMEM((CHANNELS, RANK), F32),
            pltpu.SMEM((1, 1, LEVELS, 2), jnp.int32),
            pltpu.VMEM((128, 192), F32), pltpu.VMEM((64, 384), F32), pltpu.VMEM((4 * LEVELS, 256, 256), BF),
            pltpu.VMEM((128, 192), BF), pltpu.VMEM((64, 384), BF),
            strips, field, strips, strips,
            pltpu.VMEM((CHANNELS // 2, 192, 256), BF), pltpu.VMEM((GROUPS // 2, 192, 256), BF),
            pltpu.VMEM((LEVELS, 64 * PER, 512), BF), pltpu.VMEM((64 * PER, 512), BF),
            pltpu.VMEM((PER // 2, 256, 256), BF), pltpu.VMEM((PER // 8, 256, 256), BF),
            field, field, pltpu.VMEM((GROUPS, 64, COLS), F32), field, strips, strips,
            pltpu.VMEM((RANK, CHANNELS, COLS), F32),
            pltpu.VMEM((1, COLS), F32), pltpu.VMEM((fy_count, 1, COLS), F32),
            pltpu.VMEM((1, COLS), F32), pltpu.VMEM((fx_count, 1, COLS), F32),
            dma((8,)), dma((HALVES, 3)), dma((HALVES, 3)), dma((2,)), dma((2,)), dma((HALVES, 3)), dma((HALVES, 3)),
        ],
        compiler_params=pltpu.CompilerParams(collective_id=0, has_side_effects=True, vmem_limit_bytes=40 * 1024 * 1024),
        name="step",
    )(start_image, dirty, sampling, basis_seed, margin,
      jnp.asarray(forward, F32), jnp.asarray(backward, F32), jnp.asarray(column, BF))
    factor = factor[0, 0]
    return jnp.maximum(pa - factor * pb, 0.0), factor * shifted


def solution(mesh):
    fy_count, fx_count = mesh.shape["fy"], mesh.shape["fx"]

    def step(*args):
        return per_device(fy_count, fx_count, *args)

    image = P(None, "fy", "fx")
    return jax.shard_map(
        step, mesh=mesh, in_specs=(image, image, image, P(), P("fy", "fx", None, None)),
        out_specs=(image, image), check_vma=False)
```

time: 110 us -> 40.4 us (0.37); the launches traced: 108 us -> 40 us
  starting transfers between devices: 34.2 us -> 0 us
  Pallas kernels: 0 us -> 31.8 us
  waiting for transfers between devices: 25.6 us -> 0 us
  other arithmetic: 18.7 us -> 0.89 us
  matrix products: 17.4 us -> 0 us
  between operations: 6.96 us -> 0.65 us
  local copies, waits for them, and re-layouts: 5.08 us -> 6.64 us
    pallas_call x0 -> x1, Pallas kernels: none -> 31.8 us  [per_device(): pl.pallas_call(body, out_shape=(tile, tile, tile, jax.ShapeDtypeStruct((1...]
    all_to_all x2 -> x0, starting transfers between devices: 23.6 us -> none  [from_everyone(): lax.all_to_all(jnp.broadcast_to(value[None], (length, *value.shape)), axi...]
    ppermute x4 -> x0, waiting for transfers between devices: 23 us -> none  [passed_along(): lax.ppermute(value, axis, [(source, source + steps) for source in range(f...]
    dot_general x22 -> x0, matrix products: 17.4 us -> none  [the longest x2 2.33 us: analyse(): col_low = jnp.einsum('cjv,vw->cjw', extended, low_cols, precision=highest)]
    reduce_sum x10 -> x0, other arithmetic: 13.2 us -> none  [the longest x5 7.64 us: orthonormal(): vector = vector - jnp.sum(previous * vector) * previous]
    ppermute x4 -> x0, starting transfers between devices: 10.6 us -> none  [passed_along(): lax.ppermute(value, axis, [(source, source + steps) for source in range(f...]
    unnamed x11 -> x15, local copies, waits for them, and re-layouts: 1.66 us -> 6.64 us
    div x1 -> x0, other arithmetic: 3.75 us -> none  [orthonormal(): vector = vector / jnp.sqrt(jnp.sum(vector * vector))]
  transfers between devices with their start and end apart: 6 -> 0, of which waited for: 3 -> 0; matrix products, arithmetic and copies ran while one was open for 32% -> 0% of each run, Pallas kernels for 0% -> 0%
where the time goes in v1:
time: 40.4 us; the launch traced here: 40 us
  Pallas kernels  31.8 us (79%)
  local copies, waits for them, and re-layouts  6.64 us (16%)
  other arithmetic  0.89 us (2%)
  between operations  0.65 us (2%)
    pallas_call x1, Pallas kernels, per_device(): pl.pallas_call(body, out_shape=(tile, tile, tile, jax.ShapeDtypeStruct((1...  31.8 us
    unnamed x15, local copies, waits for them, and re-layouts  6.64 us
    max x1, other arithmetic, per_device(): return (jnp.maximum(pa - factor * pb, 0.0), factor * shifted)  0.89 us

profile of v1, /device:TPU:1, one launch (start us, length us, event | category | flops | bytes accessed | tf_op | source)
XLA Modules:
  0.0 40.0 jit_solution(364548621275555180)
XLA Ops:
  0.6 0.0 copy-start.6
  0.6 0.8 %copy.10.refs_3_ = f32[16,4]{1,0:T(8,128)S(1)} copy(f32[16,4]{0,1:T(4,128)} %param.11) | data formatting | bytes 512 | tf_op args[3]
  1.4 0.0 copy-done.6
  1.4 0.0 copy-start
  1.4 1.2 %copy-done = bf16[8,256,256]{2,1,0:T(8,128)(2,1)S(1)} copy-done((bf16[8,256,256]{2,1,0:T(8,128)(2,1)S(1)}, bf16[8,256,256]{2,1,0:T(8,128)(2,1)}, u32[]{:S(2)}) %copy-start) | copy-done | bytes 1048600
  2.6 0.0 copy-start.1
  2.6 0.9 %copy-done.1 = f32[16,32,128]{2,1,0:T(8,128)S(1)} copy-done((f32[16,32,128]{2,1,0:T(8,128)S(1)}, f32[16,32,128]{2,1,0:T(8,128)}, u32[]{:S(2)}) %copy-start.1) | copy-done | bytes 262168
  3.6 0.0 copy-start.2
  3.6 0.9 %copy-done.2 = f32[16,32,128]{2,1,0:T(8,128)S(1)} copy-done((f32[16,32,128]{2,1,0:T(8,128)S(1)}, f32[16,32,128]{2,1,0:T(8,128)}, u32[]{:S(2)}) %copy-start.2) | copy-done | bytes 262168
  4.5 0.0 copy-start.3
  4.5 0.9 %copy-done.3 = f32[16,32,128]{2,1,0:T(8,128)S(1)} copy-done((f32[16,32,128]{2,1,0:T(8,128)S(1)}, f32[16,32,128]{2,1,0:T(8,128)}, u32[]{:S(2)}) %copy-start.3) | copy-done | bytes 262168
  5.5 0.0 copy-start.4
  5.5 0.9 %copy-done.4 = f32[128,192]{1,0:T(8,128)S(1)} copy-done((f32[128,192]{1,0:T(8,128)S(1)}, f32[128,192]{1,0:T(8,128)}, u32[]{:S(2)}) %copy-start.4) | copy-done | bytes 98328
  6.4 0.0 copy-start.5
  6.4 0.9 %copy-done.5 = f32[64,384]{1,0:T(8,128)S(1)} copy-done((f32[64,384]{1,0:T(8,128)S(1)}, f32[64,384]{1,0:T(8,128)}, u32[]{:S(2)}) %copy-start.5) | copy-done | bytes 98328
  7.3 31.8 %step.1 = (f32[16,32,128]{2,1,0:T(8,128)S(1)}, f32[16,32,128]{2,1,0:T(8,128)S(1)}, f32[16,32,128]{2,1,0:T(8,128)S(1)}, f32[1,128]{1,0:T(1,128)S(1)}) custom-call(f32[16,32,128]{2,1,0:T(8,128)S(1)} %copy-done.1, f32[16,32,128]{2,1,0:T(8,128)S(1)} %copy-done.2, f32[16,32,128]{2,1,0:T(8,128)S(1)} %copy-done.3, f32[16,4]{1,0:T(8,128)S(1)} %copy.10.refs_3_, ...), custom_call_target="tpu_custom_call" | custom-call | tf_op jit(solution)/shard_map/step/pallas_call | solution.py:378
  39.1 0.9 %subtract_maximum_fusion = (f32[16,32,128]{2,1,0:T(8,128)}, f32[16,32,128]{2,1,0:T(8,128)}) fusion(f32[16,32,128]{2,1,0:T(8,128)S(1)} %get-tuple-element.6, f32[16,32,128]{2,1,0:T(8,128)S(1)} %get-tuple-element.8, f32[]{:T(128)S(1)} %bitcast.2, f32[16,32,128]{2,1,0:T(8,128)S(1)} %get-tuple-element.9), kind=kLoop, calls=%fused_computation | loop fusion | flops 262144 | bytes 1310724 | tf_op jit(solution)/shard_map/max | solution.py:404
Async XLA Ops:
  0.6 0.8 %copy-start.6 = (s32[1,1,2,2]{3,2,1,0:T(2,128)S(1)}, s32[1,1,2,2]{3,2,1,0:T(2,128)}, u32[]{:S(2)}) copy-start(s32[1,1,2,2]{3,2,1,0:T(2,128)} %refs_4_.1) | copy-start | bytes 52
  1.4 1.2 %copy-start = (bf16[8,256,256]{2,1,0:T(8,128)(2,1)S(1)}, bf16[8,256,256]{2,1,0:T(8,128)(2,1)}, u32[]{:S(2)}) copy-start(bf16[8,256,256]{2,1,0:T(8,128)(2,1)} %constant.10.clone.refs_7_) | copy-start | bytes 3145732
  2.6 0.9 %copy-start.1 = (f32[16,32,128]{2,1,0:T(8,128)S(1)}, f32[16,32,128]{2,1,0:T(8,128)}, u32[]{:S(2)}) copy-start(f32[16,32,128]{2,1,0:T(8,128)} %refs_0_.1) | copy-start | bytes 786436
  3.6 0.9 %copy-start.2 = (f32[16,32,128]{2,1,0:T(8,128)S(1)}, f32[16,32,128]{2,1,0:T(8,128)}, u32[]{:S(2)}) copy-start(f32[16,32,128]{2,1,0:T(8,128)} %refs_1_.1) | copy-start | bytes 786436
  4.5 0.9 %copy-start.3 = (f32[16,32,128]{2,1,0:T(8,128)S(1)}, f32[16,32,128]{2,1,0:T(8,128)}, u32[]{:S(2)}) copy-start(f32[16,32,128]{2,1,0:T(8,128)} %refs_2_.1) | copy-start | bytes 786436
  5.5 0.9 %copy-start.4 = (f32[128,192]{1,0:T(8,128)S(1)}, f32[128,192]{1,0:T(8,128)}, u32[]{:S(2)}) copy-start(f32[128,192]{1,0:T(8,128)} %constant.8.clone.refs_5_) | copy-start | bytes 294916
  6.4 0.9 %copy-start.5 = (f32[64,384]{1,0:T(8,128)S(1)}, f32[64,384]{1,0:T(8,128)}, u32[]{:S(2)}) copy-start(f32[64,384]{1,0:T(8,128)} %constant.9.clone.refs_6_) | copy-start | bytes 294916

commit v2 on v1

--- a/solution.py
+++ b/solution.py
@@ -105,7 +105,7 @@
                 fwd_m, bwd_m, pack, above, left_in, corner_in,
                 x_own, x_left, lhs, bands, z_own, z_left, own, up_out, left_out, up_in, left_back, corner_back,
                 spec, e_send, e_recv, f_send, f_recv,
-                load_sem, halo_send, halo_recv, e_sem, f_sem, back_send, back_recv):
+                load_sem, halo_send, halo_recv, e_sem, f_sem, back_send, back_recv, far_sem):
     me_y, me_x = lax.axis_index("fy"), lax.axis_index("fx")
     below, over = lax.rem(me_y + 1, fy_count), lax.rem(me_y + fy_count - 1, fy_count)
     right, left = lax.rem(me_x + 1, fx_count), lax.rem(me_x + fx_count - 1, fx_count)
@@ -130,8 +130,10 @@
         greet({"fy": lax.rem(me_y + k, fy_count), "fx": me_x})
         return carry
 
-    lax.fori_loop(1, fx_count, greet_x, 0)
+    near = fx_count // 4
     lax.fori_loop(1, fy_count, greet_y, 0)
+    lax.fori_loop(1, near + 1, greet_x, 0)
+    lax.fori_loop(fx_count - near, fx_count, greet_x, 0)
     greet({"fy": below, "fx": right})
     greet({"fy": over, "fx": left})
 
@@ -157,7 +159,9 @@
     e_send[...] = energy
     e_recv[me_y] = energy
 
-    pl.semaphore_wait(barrier, fx_count + fy_count)
+    pl.semaphore_wait(barrier, fy_count - 1 + 2 * near + 2)
+    for device in (near, fx_count - near):
+        pl.semaphore_signal(far_sem, inc=1, device_id={"fy": me_y, "fx": lax.rem(me_x + device, fx_count)}, device_id_type=MESH)
 
     def energy_copy(k):
         return pltpu.make_async_remote_copy(
@@ -207,8 +211,10 @@
         kept.append([jnp.logical_and(inside, block == q) for q in range(4)])
 
     columns = []
+    diagonal = lax.broadcasted_iota(jnp.int32, (CHANNELS, CHANNELS), 0) == lax.broadcasted_iota(jnp.int32, (CHANNELS, CHANNELS), 1)
     for r in range(RANK):
-        vector = jnp.broadcast_to(basis[:, r : r + 1], (CHANNELS, COLS))
+        vector = jnp.sum(jnp.where(diagonal, basis[r : r + 1, :], 0.0), axis=1, keepdims=True)
+        vector = jnp.broadcast_to(vector, (CHANNELS, COLS))
         for previous in columns:
             vector = vector - jnp.sum(previous * vector, axis=0, keepdims=True) * previous
         vector = vector / jnp.sqrt(jnp.sum(vector * vector, axis=0, keepdims=True))
@@ -249,6 +255,8 @@
     partial = jnp.sum(e_recv[...], axis=0)
     f_send[...] = partial
     f_recv[me_x] = partial
+
+    pl.semaphore_wait(far_sem, 2)
 
     def second_start(k, carry):
         pltpu.make_async_remote_copy(
@@ -382,7 +390,7 @@
         out_specs=(vmem,) * 4,
         scratch_shapes=[
             field, field, field,
-            pltpu.VMEM((CHANNELS, RANK), F32),
+            pltpu.VMEM((RANK, CHANNELS), F32),
             pltpu.SMEM((1, 1, LEVELS, 2), jnp.int32),
             pltpu.VMEM((128, 192), F32), pltpu.VMEM((64, 384), F32), pltpu.VMEM((4 * LEVELS, 256, 256), BF),
             pltpu.VMEM((128, 192), BF), pltpu.VMEM((64, 384), BF),
@@ -395,11 +403,13 @@
             pltpu.VMEM((1, COLS), F32), pltpu.VMEM((fy_count, 1, COLS), F32),
             pltpu.VMEM((1, COLS), F32), pltpu.VMEM((fx_count, 1, COLS), F32),
             dma((8,)), dma((HALVES, 3)), dma((HALVES, 3)), dma((2,)), dma((2,)), dma((HALVES, 3)), dma((HALVES, 3)),
+            pltpu.SemaphoreType.REGULAR,
         ],
         compiler_params=pltpu.CompilerParams(collective_id=0, has_side_effects=True, vmem_limit_bytes=40 * 1024 * 1024),
         name="step",
-    )(start_image, dirty, sampling, basis_seed, margin,
-      jnp.asarray(forward, F32), jnp.asarray(backward, F32), jnp.asarray(column, BF))
+    )(*(pltpu.with_memory_space_constraint(value, pltpu.HBM) for value in (
+        start_image, dirty, sampling, basis_seed.T, margin,
+        jnp.asarray(forward, F32), jnp.asarray(backward, F32), jnp.asarray(column, BF))))
     factor = factor[0, 0]
     return jnp.maximum(pa - factor * pb, 0.0), factor * shifted
 

time: 40.4 us -> 30.6 us (0.76)
  local copies, waits for them, and re-layouts: 6.64 us -> 0 us
  Pallas kernels: 31.8 us -> 28.9 us
    unnamed x15 -> x0, local copies, waits for them, and re-layouts: 6.64 us -> none
    pallas_call x1, Pallas kernels: 31.8 us -> 28.9 us  [per_device(): pl.pallas_call(body, out_shape=(tile, tile, tile, jax.ShapeDtypeStruct((1...]
where the time goes in v2:
time: 30.6 us; the launch traced here: 30.4 us
  Pallas kernels  28.9 us (94%)
  other arithmetic  0.89 us (3%)
  between operations  0.64 us (2%)
    pallas_call x1, Pallas kernels, per_device(): pl.pallas_call(body, out_shape=(tile, tile, tile, jax.ShapeDtypeStruct((1...  28.9 us
    max x1, other arithmetic, per_device(): return (jnp.maximum(pa - factor * pb, 0.0), factor * shifted)  0.89 us

profile of v2, /device:TPU:1, one launch (start us, length us, event | category | flops | bytes accessed | tf_op | source)
XLA Modules:
  0.0 30.4 jit_solution(16023852722980200628)
XLA Ops:
  0.6 28.9 %step.1 = (f32[16,32,128]{2,1,0:T(8,128)S(1)}, f32[16,32,128]{2,1,0:T(8,128)S(1)}, f32[16,32,128]{2,1,0:T(8,128)S(1)}, f32[1,128]{1,0:T(1,128)S(1)}) custom-call(f32[16,32,128]{2,1,0:T(8,128)} %refs_0_.1, f32[16,32,128]{2,1,0:T(8,128)} %refs_1_.1, f32[16,32,128]{2,1,0:T(8,128)} %refs_2_.1, f32[4,16]{1,0:T(4,128)} %bitcast.4, s32[1,1,2,2]{3,2,1,0:T(2,128)} %refs_4_.1, ...), custom_call_target="tpu_custom_call" | custom-call | tf_op jit(solution)/shard_map/step/pallas_call | solution.py:386
  29.5 0.9 %subtract_maximum_fusion = (f32[16,32,128]{2,1,0:T(8,128)}, f32[16,32,128]{2,1,0:T(8,128)}) fusion(f32[16,32,128]{2,1,0:T(8,128)S(1)} %get-tuple-element.6, f32[16,32,128]{2,1,0:T(8,128)S(1)} %get-tuple-element.8, f32[]{:T(128)S(1)} %bitcast.3, f32[16,32,128]{2,1,0:T(8,128)S(1)} %get-tuple-element.9), kind=kLoop, calls=%fused_computation | loop fusion | flops 262144 | bytes 1310724 | tf_op jit(solution)/shard_map/max | solution.py:414

commit v3 on v2

--- a/solution.py
+++ b/solution.py
@@ -1,3 +1,4 @@
+import functools
 import math
 
 import jax
@@ -19,6 +20,7 @@
 CHANNELS = 16
 RANK = 4
 HALVES = 2
+EARLY = 4
 PER = CHANNELS // HALVES
 GROUPS = CHANNELS // 4
 
@@ -84,9 +86,9 @@
     backward = np.concatenate([hi.T, hi.T, lo.T], axis=1)
     column = []
     for level in range(LEVELS):
-        column.extend(split_host(cols[level]))
+        column.append(split_host(cols[level])[0])
     for level in range(LEVELS):
-        column.extend(split_host(cols[level].T))
+        column.append(split_host(cols[level].T)[0])
     return forward, backward, np.stack(column)
 
 
@@ -104,8 +106,8 @@
                 start, dirty, samp, basis, margin, fwd_raw, bwd_raw, col,
                 fwd_m, bwd_m, pack, above, left_in, corner_in,
                 x_own, x_left, lhs, bands, z_own, z_left, own, up_out, left_out, up_in, left_back, corner_back,
-                spec, e_send, e_recv, f_send, f_recv,
-                load_sem, halo_send, halo_recv, e_sem, f_sem, back_send, back_recv, far_sem):
+                spec, line_out, line_in, plane_out, plane_in, total_out, total_in,
+                load_sem, halo_send, halo_recv, line_sem, plane_sem, total_sem, back_send, back_recv):
     me_y, me_x = lax.axis_index("fy"), lax.axis_index("fx")
     below, over = lax.rem(me_y + 1, fy_count), lax.rem(me_y + fy_count - 1, fy_count)
     right, left = lax.rem(me_x + 1, fx_count), lax.rem(me_x + fx_count - 1, fx_count)
@@ -113,34 +115,63 @@
     loads = []
     for at, (source, target) in enumerate([(start_hbm, start), (dirty_hbm, dirty), (samp_hbm, samp), (margin_hbm, margin),
                                            (basis_hbm, basis), (fwd_hbm, fwd_raw), (bwd_hbm, bwd_raw), (col_hbm, col)]):
-        copy = pltpu.make_async_copy(source, target, load_sem.at[at])
+        loads.append(pltpu.make_async_copy(source, target, load_sem.at[at]))
+    for copy in loads[:3]:
         copy.start()
-        loads.append(copy)
 
     barrier = pltpu.get_barrier_semaphore()
 
     def greet(device):
         pl.semaphore_signal(barrier, inc=1, device_id=device, device_id_type=MESH)
 
-    def greet_x(k, carry):
-        greet({"fy": me_y, "fx": lax.rem(me_x + k, fx_count)})
-        return carry
-
-    def greet_y(k, carry):
-        greet({"fy": lax.rem(me_y + k, fy_count), "fx": me_x})
-        return carry
-
-    near = fx_count // 4
-    lax.fori_loop(1, fy_count, greet_y, 0)
-    lax.fori_loop(1, near + 1, greet_x, 0)
-    lax.fori_loop(fx_count - near, fx_count, greet_x, 0)
-    greet({"fy": below, "fx": right})
-    greet({"fy": over, "fx": left})
+    row, chip, core = me_y // 8, lax.rem(me_y // 2, 4), lax.rem(me_y, 2)
+    plane = []
+    for far in (4, 3, 2, 1, 0):
+        for dy in range(4):
+            for dx in range(4):
+                for dc in range(2):
+                    if min(dy, 4 - dy) + min(dx, 4 - dx) == far and (dy, dx, dc) != (0, 0, 0):
+                        at = 8 * lax.rem(row + dy, 4) + 2 * lax.rem(chip + dx, 4) + lax.rem(core + dc, 2)
+                        plane.append({"fy": at, "fx": me_x})
+    line = {}
+    for k in range(1, fx_count):
+        line[k] = {"fy": me_y, "fx": lax.rem(me_x + k, fx_count)}
+    order = sorted(line, key=lambda k: -min(k, fx_count - k))
+    is_early, is_late = me_x < EARLY, me_x >= EARLY
+    has_left, has_right = me_x > 0, me_x < fx_count - 1
+
+    def greet_many():
+        for k in order:
+            greet(line[k])
+        for device in plane:
+            greet(device)
+
+    def greet_few():
+        greet({"fy": over, "fx": me_x})
+        greet({"fy": below, "fx": me_x})
+        greet({"fy": me_y, "fx": left})
+
+    pl.when(is_early)(greet_many)
+    pl.when(is_late)(greet_few)
+    pl.when(jnp.logical_and(is_late, has_right))(lambda: greet({"fy": me_y, "fx": right}))
+    pl.when(has_right)(lambda: greet({"fy": below, "fx": right}))
+    pl.when(has_left)(lambda: greet({"fy": over, "fx": left}))
 
     lane = lax.broadcasted_iota(jnp.int32, (1, COLS), 1)
     block = lane // PAD
 
-    loads[0].wait()
+    for copy in loads[:3]:
+        copy.wait()
+    for copy in loads[3:]:
+        copy.start()
+    energy = jnp.zeros((ROWS, COLS), F32)
+    for c in range(CHANNELS):
+        value = DUAL_STEP * samp[c] * start[c] - DUAL_STEP * dirty[c]
+        shifted_ref[c] = value
+        energy = energy + value * value
+    energy = jnp.sum(energy, axis=0, keepdims=True)
+    line_out[...] = energy
+
     for g in range(GROUPS):
         total = jnp.zeros((ROWS, COLS), F32)
         for q in range(4):
@@ -148,31 +179,20 @@
             moved = value if q == 3 else pltpu.roll(value, PAD * (q + 1), 1)
             total = jnp.where(block == q, moved, total)
         pack[g] = total
-    loads[1].wait()
-    loads[2].wait()
-    energy = jnp.zeros((ROWS, COLS), F32)
-    for c in range(CHANNELS):
-        value = DUAL_STEP * samp[c] * start[c] - DUAL_STEP * dirty[c]
-        shifted_ref[c] = value
-        energy = energy + value * value
-    energy = jnp.sum(energy, axis=0, keepdims=True)
-    e_send[...] = energy
-    e_recv[me_y] = energy
-
-    pl.semaphore_wait(barrier, fy_count - 1 + 2 * near + 2)
-    for device in (near, fx_count - near):
-        pl.semaphore_signal(far_sem, inc=1, device_id={"fy": me_y, "fx": lax.rem(me_x + device, fx_count)}, device_id_type=MESH)
-
-    def energy_copy(k):
+    one = lambda flag: flag.astype(jnp.int32)
+    guests = jnp.where(
+        is_early,
+        len(plane) + EARLY - 1 + one(me_x == EARLY - 1) + one(has_left) + 1,
+        2 + EARLY + one(me_x > EARLY) + 1 + 2 * one(has_right))
+    pl.semaphore_wait(barrier, guests)
+
+    def line_copy(z):
         return pltpu.make_async_remote_copy(
-            src_ref=e_send, dst_ref=e_recv.at[me_y], send_sem=e_sem.at[0], recv_sem=e_sem.at[1],
-            device_id={"fy": lax.rem(me_y + k, fy_count), "fx": me_x}, device_id_type=MESH)
-
-    def energy_start(k, carry):
-        energy_copy(k).start()
-        return carry
-
-    lax.fori_loop(1, fy_count, energy_start, 0)
+            src_ref=line_out, dst_ref=line_in.at[me_x], send_sem=line_sem.at[0], recv_sem=line_sem.at[1],
+            device_id={"fy": me_y, "fx": z}, device_id_type=MESH)
+
+    for z in range(EARLY):
+        pl.when(me_x != z)(lambda z=z: line_copy(z).start())
 
     halos = []
     for h in range(HALVES):
@@ -186,8 +206,22 @@
             copy = pltpu.make_async_remote_copy(
                 src_ref=source, dst_ref=target, send_sem=halo_send.at[h, at], recv_sem=halo_recv.at[h, at],
                 device_id=device, device_id_type=MESH)
-            copy.start()
+            if at == 0:
+                copy.start()
+            else:
+                pl.when(has_right)(copy.start)
             halos.append(copy)
+
+    def no_left():
+        left_in[...] = jnp.zeros_like(left_in)
+        corner_in[...] = jnp.zeros_like(corner_in)
+
+    def no_right():
+        left_back[...] = jnp.zeros_like(left_back)
+        corner_back[...] = jnp.zeros_like(corner_back)
+
+    pl.when(jnp.logical_not(has_left))(no_left)
+    pl.when(jnp.logical_not(has_right))(no_right)
 
     for copy in loads[3:]:
         copy.wait()
@@ -251,31 +285,21 @@
     for c in range(CHANNELS):
         place(x_own, c // 2, c % 2, PAD, start[c])
 
-    pltpu.make_async_copy(e_recv.at[pl.ds(0, fy_count - 1)], e_recv.at[pl.ds(0, fy_count - 1)], e_sem.at[1]).wait()
-    partial = jnp.sum(e_recv[...], axis=0)
-    f_send[...] = partial
-    f_recv[me_x] = partial
-
-    pl.semaphore_wait(far_sem, 2)
-
-    def second_start(k, carry):
-        pltpu.make_async_remote_copy(
-            src_ref=f_send, dst_ref=f_recv.at[me_x], send_sem=f_sem.at[0], recv_sem=f_sem.at[1],
-            device_id={"fy": me_y, "fx": lax.rem(me_x + k, fx_count)}, device_id_type=MESH).start()
-        return carry
-
-    lax.fori_loop(1, fx_count, second_start, 0)
-
     backs = []
     for h in range(HALVES):
-        for copy in halos[3 * h : 3 * h + 3]:
-            copy.wait_recv()
+        halos[3 * h].wait_recv()
+
+        def from_left(h=h):
+            halos[3 * h + 1].wait_recv()
+            halos[3 * h + 2].wait_recv()
+
+        pl.when(has_left)(from_left)
         first = h * PER
         for c in range(first, first + PER):
             place(x_own, c // 2, c % 2, 0, above[c])
         for g in range(first // 4, (first + PER) // 4):
-            place(x_left, g // 2, g % 2, 0, corner_in[g])
-            place(x_left, g // 2, g % 2, PAD, left_in[g])
+            place(x_left, g, 0, 0, corner_in[g])
+            place(x_left, g, 0, PAD, left_in[g])
         for p in range(first // 2, (first + PER) // 2):
             u = dot(fwd_m[...], x_own[p])
             high, low = split(u)
@@ -285,19 +309,17 @@
                 for l in range(LEVELS):
                     lhs[l, pl.ds(64 * c, 64), 0:128] = high[64 * l : 64 * l + 64, lanes]
                     lhs[l, pl.ds(64 * c, 64), 256:384] = low[64 * l : 64 * l + 64, lanes]
-        for p in range(first // 8, (first + PER) // 8):
-            u = dot(fwd_m[...], x_left[p])
-            for part in range(2):
-                for q in range(4):
-                    c = 8 * p + 4 * part + q - first
-                    for l in range(LEVELS):
-                        value = jnp.where(kept[l][q], u[64 * l : 64 * l + 64, COLS * part : COLS * (part + 1)], 0.0)
-                        high, low = split(value)
-                        lhs[l, pl.ds(64 * c, 64), 128:256] = high
-                        lhs[l, pl.ds(64 * c, 64), 384:512] = low
+        for g in range(first // 4, (first + PER) // 4):
+            u = dot(fwd_m[...], x_left[g])
+            for q in range(4):
+                c = 4 * g + q - first
+                for l in range(LEVELS):
+                    high, low = split(jnp.where(kept[l][q], u[64 * l : 64 * l + 64, :], 0.0))
+                    lhs[l, pl.ds(64 * c, 64), 128:256] = high
+                    lhs[l, pl.ds(64 * c, 64), 384:512] = low
         z_sum = [[jnp.zeros((64, COLS), F32) for l in range(LEVELS)] for g in range(PER // 4)]
         for l in range(LEVELS):
-            acc = dot(lhs[l, :, 0:256], col[2 * l]) + dot(lhs[l, :, 256:512], col[2 * l]) + dot(lhs[l, :, 0:256], col[2 * l + 1])
+            acc = dot(lhs[l, :, 0:256], col[l]) + dot(lhs[l, :, 256:512], col[l])
             acc = jnp.clip(acc, -CLIP_LEVEL, CLIP_LEVEL)
             high, low = split(acc)
             for c in range(PER):
@@ -309,8 +331,7 @@
                 bands[pl.ds(top, 32), 384:512] = low[top:mid, 128:256]
                 bands[pl.ds(mid, 32), 0:256] = high[mid:end, :]
                 bands[pl.ds(mid, 32), 256:512] = low[mid:end, :]
-            at = 2 * LEVELS + 2 * l
-            z = dot(bands[:, 0:256], col[at]) + dot(bands[:, 256:512], col[at]) + dot(bands[:, 0:256], col[at + 1])
+            z = dot(bands[:, 0:256], col[LEVELS + l]) + dot(bands[:, 256:512], col[LEVELS + l])
             for c in range(PER):
                 high, low = split(z[64 * c : 64 * c + 64, 0:128])
                 lanes = pl.ds(COLS * (c % 2), COLS)
@@ -319,15 +340,11 @@
                 piece = z[64 * c : 64 * c + 64, 128:256]
                 z_sum[c // 4][l] = z_sum[c // 4][l] + jnp.where(kept[l][c % 4], piece, 0.0)
         for g in range(PER // 4):
-            lanes = pl.ds(COLS * (g % 2), COLS)
             for l in range(LEVELS):
                 high, low = split(z_sum[g][l])
-                z_left[g // 2, pl.ds(64 * l, 64), lanes] = high
-                z_left[g // 2, pl.ds(128 + 64 * l, 64), lanes] = low
-        for p in range(PER // 8):
-            r = dot(bwd_m[:, 0:256], z_left[p]) + dot(bwd_m[:, 256:384], z_left[p, 0:128, :])
-            for part in range(2):
-                left_out[first // 4 + 2 * p + part] = r[:, COLS * part : COLS * (part + 1)]
+                z_left[g, pl.ds(64 * l, 64), :] = high
+                z_left[g, pl.ds(128 + 64 * l, 64), :] = low
+            left_out[first // 4 + g] = dot(bwd_m[:, 0:256], z_left[g]) + dot(bwd_m[:, 256:384], z_left[g, 0:128, :])
         for p in range(PER // 2):
             r = dot(bwd_m[:, 0:256], z_own[p]) + dot(bwd_m[:, 256:384], z_own[p, 0:128, :])
             for part in range(2):
@@ -344,11 +361,30 @@
             copy = pltpu.make_async_remote_copy(
                 src_ref=source, dst_ref=target, send_sem=back_send.at[h, at], recv_sem=back_recv.at[h, at],
                 device_id=device, device_id_type=MESH)
-            copy.start()
+            if at == 2:
+                copy.start()
+            else:
+                pl.when(has_left)(copy.start)
             backs.append(copy)
 
-    for copy in backs:
-        copy.wait_recv()
+    def exchange():
+        pltpu.make_async_copy(line_in.at[pl.ds(0, fx_count - 1)], line_in.at[pl.ds(0, fx_count - 1)], line_sem.at[1]).wait()
+        line_in[me_x] = line_out[...]
+        partial = jnp.sum(line_in[...], axis=0)
+        plane_out[...] = partial
+        plane_in[me_y] = partial
+        for device in plane:
+            pltpu.make_async_remote_copy(
+                src_ref=plane_out, dst_ref=plane_in.at[me_y], send_sem=plane_sem.at[0], recv_sem=plane_sem.at[1],
+                device_id=device, device_id_type=MESH).start()
+
+    pl.when(is_early)(exchange)
+
+    for at, copy in enumerate(backs):
+        if at % 3 == 2:
+            copy.wait_recv()
+        else:
+            pl.when(has_right)(copy.wait_recv)
     for g in range(GROUPS):
         strip = left_back[g] + corner_back[g]
         for q in range(4):
@@ -359,16 +395,55 @@
     for c in range(CHANNELS):
         pa_ref[c] = pa(c)
 
-    pltpu.make_async_copy(f_recv.at[pl.ds(0, fx_count - 1)], f_recv.at[pl.ds(0, fx_count - 1)], f_sem.at[1]).wait()
-    total = jnp.sum(jnp.sum(f_recv[...], axis=0), axis=1, keepdims=True)
+    def total_copy(z):
+        return pltpu.make_async_remote_copy(
+            src_ref=total_out, dst_ref=total_in, send_sem=total_sem.at[0], recv_sem=total_sem.at[1],
+            device_id={"fy": me_y, "fx": z}, device_id_type=MESH)
+
+    middle = (EARLY - 1 + fx_count) // 2 + 1
+    shares = {0: range(fx_count - 1, middle - 1, -1), EARLY - 1: range(EARLY, middle)}
+
+    def finish():
+        pltpu.make_async_copy(plane_in.at[pl.ds(0, fy_count - 1)], plane_in.at[pl.ds(0, fy_count - 1)], plane_sem.at[1]).wait()
+        total = jnp.sum(plane_in[...], axis=0)
+        total_in[...] = total
+        total_out[...] = total
+
+    def hand(zs):
+        for z in zs:
+            total_copy(z).start()
+
+    pl.when(is_early)(finish)
+    for z, zs in shares.items():
+        pl.when(me_x == z)(functools.partial(hand, zs))
+    pl.when(is_late)(lambda: total_copy(0).wait_recv())
+    total = jnp.sum(total_in[...], axis=1, keepdims=True)
     radius = BALL_SCALE * math.sqrt(CHANNELS * ROWS * COLS * fy_count * fx_count)
     factor = jnp.maximum(0.0, 1.0 - DUAL_STEP * radius / jnp.sqrt(total + NORM_EPS))
     factor_ref[...] = jnp.broadcast_to(factor, (1, COLS))
 
-    for copy in halos + backs:
-        copy.wait_send()
-    pltpu.make_async_copy(e_recv.at[pl.ds(0, fy_count - 1)], e_recv.at[pl.ds(0, fy_count - 1)], e_sem.at[0]).wait()
-    pltpu.make_async_copy(f_recv.at[pl.ds(0, fx_count - 1)], f_recv.at[pl.ds(0, fx_count - 1)], f_sem.at[0]).wait()
+    for at, copy in enumerate(halos):
+        if at % 3 == 0:
+            copy.wait_send()
+        else:
+            pl.when(has_right)(copy.wait_send)
+    for at, copy in enumerate(backs):
+        if at % 3 == 2:
+            copy.wait_send()
+        else:
+            pl.when(has_left)(copy.wait_send)
+
+    def sent(ref, count, sem):
+        pltpu.make_async_copy(ref.at[pl.ds(0, count)], ref.at[pl.ds(0, count)], sem).wait()
+
+    def early_sent():
+        sent(line_in, EARLY - 1, line_sem.at[0])
+        sent(plane_in, fy_count - 1, plane_sem.at[0])
+
+    pl.when(is_early)(early_sent)
+    pl.when(is_late)(lambda: sent(line_in, EARLY, line_sem.at[0]))
+    for z, zs in shares.items():
+        pl.when(me_x == z)(functools.partial(sent, line_in, len(zs), total_sem.at[0]))
 
 
 def per_device(fy_count, fx_count, start_image, dirty, sampling, basis_seed, margin):
@@ -392,18 +467,18 @@
             field, field, field,
             pltpu.VMEM((RANK, CHANNELS), F32),
             pltpu.SMEM((1, 1, LEVELS, 2), jnp.int32),
-            pltpu.VMEM((128, 192), F32), pltpu.VMEM((64, 384), F32), pltpu.VMEM((4 * LEVELS, 256, 256), BF),
+            pltpu.VMEM((128, 192), F32), pltpu.VMEM((64, 384), F32), pltpu.VMEM((2 * LEVELS, 256, 256), BF),
             pltpu.VMEM((128, 192), BF), pltpu.VMEM((64, 384), BF),
             strips, field, strips, strips,
-            pltpu.VMEM((CHANNELS // 2, 192, 256), BF), pltpu.VMEM((GROUPS // 2, 192, 256), BF),
+            pltpu.VMEM((CHANNELS // 2, 192, 256), BF), pltpu.VMEM((GROUPS, 192, COLS), BF),
             pltpu.VMEM((LEVELS, 64 * PER, 512), BF), pltpu.VMEM((64 * PER, 512), BF),
-            pltpu.VMEM((PER // 2, 256, 256), BF), pltpu.VMEM((PER // 8, 256, 256), BF),
+            pltpu.VMEM((PER // 2, 256, 256), BF), pltpu.VMEM((PER // 4, 256, COLS), BF),
             field, field, pltpu.VMEM((GROUPS, 64, COLS), F32), field, strips, strips,
             pltpu.VMEM((RANK, CHANNELS, COLS), F32),
+            pltpu.VMEM((1, COLS), F32), pltpu.VMEM((fx_count, 1, COLS), F32),
             pltpu.VMEM((1, COLS), F32), pltpu.VMEM((fy_count, 1, COLS), F32),
-            pltpu.VMEM((1, COLS), F32), pltpu.VMEM((fx_count, 1, COLS), F32),
-            dma((8,)), dma((HALVES, 3)), dma((HALVES, 3)), dma((2,)), dma((2,)), dma((HALVES, 3)), dma((HALVES, 3)),
-            pltpu.SemaphoreType.REGULAR,
+            pltpu.VMEM((1, COLS), F32), pltpu.VMEM((1, COLS), F32),
+            dma((8,)), dma((HALVES, 3)), dma((HALVES, 3)), dma((2,)), dma((2,)), dma((2,)), dma((HALVES, 3)), dma((HALVES, 3)),
         ],
         compiler_params=pltpu.CompilerParams(collective_id=0, has_side_effects=True, vmem_limit_bytes=40 * 1024 * 1024),
         name="step",

time: 30.6 us -> 28.2 us (0.922)
  Pallas kernels: 28.9 us -> 26.5 us
    pallas_call x1, Pallas kernels: 28.9 us -> 26.5 us  [per_device(): pl.pallas_call(body, out_shape=(tile, tile, tile, jax.ShapeDtypeStruct((1...]
where the time goes in v3:
time: 28.2 us; the launch traced here: 28 us
  Pallas kernels  26.5 us (94%)
  other arithmetic  0.89 us (3%)
  between operations  0.64 us (2%)
    pallas_call x1, Pallas kernels, per_device(): pl.pallas_call(body, out_shape=(tile, tile, tile, jax.ShapeDtypeStruct((1...  26.5 us
    max x1, other arithmetic, per_device(): return (jnp.maximum(pa - factor * pb, 0.0), factor * shifted)  0.89 us

profile of v3, /device:TPU:1, one launch (start us, length us, event | category | flops | bytes accessed | tf_op | source)
XLA Modules:
  0.0 28.0 jit_solution(7794346886898878408)
XLA Ops:
  0.6 26.5 %step.1 = (f32[16,32,128]{2,1,0:T(8,128)S(1)}, f32[16,32,128]{2,1,0:T(8,128)S(1)}, f32[16,32,128]{2,1,0:T(8,128)S(1)}, f32[1,128]{1,0:T(1,128)S(1)}) custom-call(f32[16,32,128]{2,1,0:T(8,128)} %refs_0_.1, f32[16,32,128]{2,1,0:T(8,128)} %refs_1_.1, f32[16,32,128]{2,1,0:T(8,128)} %refs_2_.1, f32[4,16]{1,0:T(4,128)} %bitcast.4, s32[1,1,2,2]{3,2,1,0:T(2,128)} %refs_4_.1, ...), custom_call_target="tpu_custom_call" | custom-call | tf_op jit(solution)/shard_map/step/pallas_call | solution.py:461
  27.2 0.9 %subtract_maximum_fusion = (f32[16,32,128]{2,1,0:T(8,128)}, f32[16,32,128]{2,1,0:T(8,128)}) fusion(f32[16,32,128]{2,1,0:T(8,128)S(1)} %get-tuple-element.6, f32[16,32,128]{2,1,0:T(8,128)S(1)} %get-tuple-element.8, f32[]{:T(128)S(1)} %bitcast.3, f32[16,32,128]{2,1,0:T(8,128)S(1)} %get-tuple-element.9), kind=kLoop, calls=%fused_computation | loop fusion | flops 262144 | bytes 1310724 | tf_op jit(solution)/shard_map/max | solution.py:489

commit v4 on v3

--- a/solution.py
+++ b/solution.py
@@ -107,17 +107,22 @@
                 fwd_m, bwd_m, pack, above, left_in, corner_in,
                 x_own, x_left, lhs, bands, z_own, z_left, own, up_out, left_out, up_in, left_back, corner_back,
                 spec, line_out, line_in, plane_out, plane_in, total_out, total_in,
-                load_sem, halo_send, halo_recv, line_sem, plane_sem, total_sem, back_send, back_recv):
+                input_sem, load_sem, halo_send, halo_recv, line_sem, plane_sem, total_sem, back_send, back_recv):
     me_y, me_x = lax.axis_index("fy"), lax.axis_index("fx")
     below, over = lax.rem(me_y + 1, fy_count), lax.rem(me_y + fy_count - 1, fy_count)
     right, left = lax.rem(me_x + 1, fx_count), lax.rem(me_x + fx_count - 1, fx_count)
 
     loads = []
-    for at, (source, target) in enumerate([(start_hbm, start), (dirty_hbm, dirty), (samp_hbm, samp), (margin_hbm, margin),
-                                           (basis_hbm, basis), (fwd_hbm, fwd_raw), (bwd_hbm, bwd_raw), (col_hbm, col)]):
+    for at, (source, target) in enumerate([(margin_hbm, margin), (basis_hbm, basis), (fwd_hbm, fwd_raw), (bwd_hbm, bwd_raw), (col_hbm, col)]):
         loads.append(pltpu.make_async_copy(source, target, load_sem.at[at]))
-    for copy in loads[:3]:
-        copy.start()
+    quarters = []
+    for part in range(4):
+        chans = pl.ds(4 * part, 4)
+        quarters.append([])
+        for at, (source, target) in enumerate([(start_hbm, start), (dirty_hbm, dirty), (samp_hbm, samp)]):
+            copy = pltpu.make_async_copy(source.at[chans], target.at[chans], input_sem.at[part, at])
+            copy.start()
+            quarters[part].append(copy)
 
     barrier = pltpu.get_barrier_semaphore()
 
@@ -160,18 +165,34 @@
     lane = lax.broadcasted_iota(jnp.int32, (1, COLS), 1)
     block = lane // PAD
 
-    for copy in loads[:3]:
-        copy.wait()
-    for copy in loads[3:]:
-        copy.start()
     energy = jnp.zeros((ROWS, COLS), F32)
     for c in range(CHANNELS):
+        if c % 4 == 0:
+            for copy in quarters[c // 4]:
+                copy.wait()
         value = DUAL_STEP * samp[c] * start[c] - DUAL_STEP * dirty[c]
         shifted_ref[c] = value
         energy = energy + value * value
     energy = jnp.sum(energy, axis=0, keepdims=True)
     line_out[...] = energy
 
+    one = lambda flag: flag.astype(jnp.int32)
+    guests = jnp.where(
+        is_early,
+        len(plane) + EARLY - 1 + one(me_x == EARLY - 1) + one(has_left) + 1,
+        2 + EARLY + one(me_x > EARLY) + 1 + 2 * one(has_right))
+    pl.semaphore_wait(barrier, guests)
+
+    def line_copy(z):
+        return pltpu.make_async_remote_copy(
+            src_ref=line_out, dst_ref=line_in.at[me_x], send_sem=line_sem.at[0], recv_sem=line_sem.at[1],
+            device_id={"fy": me_y, "fx": z}, device_id_type=MESH)
+
+    for z in range(EARLY):
+        pl.when(me_x != z)(lambda z=z: line_copy(z).start())
+
+    for copy in loads:
+        copy.start()
     for g in range(GROUPS):
         total = jnp.zeros((ROWS, COLS), F32)
         for q in range(4):
@@ -179,20 +200,6 @@
             moved = value if q == 3 else pltpu.roll(value, PAD * (q + 1), 1)
             total = jnp.where(block == q, moved, total)
         pack[g] = total
-    one = lambda flag: flag.astype(jnp.int32)
-    guests = jnp.where(
-        is_early,
-        len(plane) + EARLY - 1 + one(me_x == EARLY - 1) + one(has_left) + 1,
-        2 + EARLY + one(me_x > EARLY) + 1 + 2 * one(has_right))
-    pl.semaphore_wait(barrier, guests)
-
-    def line_copy(z):
-        return pltpu.make_async_remote_copy(
-            src_ref=line_out, dst_ref=line_in.at[me_x], send_sem=line_sem.at[0], recv_sem=line_sem.at[1],
-            device_id={"fy": me_y, "fx": z}, device_id_type=MESH)
-
-    for z in range(EARLY):
-        pl.when(me_x != z)(lambda z=z: line_copy(z).start())
 
     halos = []
     for h in range(HALVES):
@@ -223,7 +230,7 @@
     pl.when(jnp.logical_not(has_left))(no_left)
     pl.when(jnp.logical_not(has_right))(no_right)
 
-    for copy in loads[3:]:
+    for copy in loads:
         copy.wait()
     row_has = (me_y > 0).astype(jnp.int32)
     col_has = (me_x > 0).astype(jnp.int32)
@@ -401,7 +408,7 @@
             device_id={"fy": me_y, "fx": z}, device_id_type=MESH)
 
     middle = (EARLY - 1 + fx_count) // 2 + 1
-    shares = {0: range(fx_count - 1, middle - 1, -1), EARLY - 1: range(EARLY, middle)}
+    shares = {EARLY - 2: range(fx_count - 1, middle, -1), EARLY - 1: range(EARLY, middle + 1)}
 
     def finish():
         pltpu.make_async_copy(plane_in.at[pl.ds(0, fy_count - 1)], plane_in.at[pl.ds(0, fy_count - 1)], plane_sem.at[1]).wait()
@@ -412,15 +419,6 @@
     def hand(zs):
         for z in zs:
             total_copy(z).start()
-
-    pl.when(is_early)(finish)
-    for z, zs in shares.items():
-        pl.when(me_x == z)(functools.partial(hand, zs))
-    pl.when(is_late)(lambda: total_copy(0).wait_recv())
-    total = jnp.sum(total_in[...], axis=1, keepdims=True)
-    radius = BALL_SCALE * math.sqrt(CHANNELS * ROWS * COLS * fy_count * fx_count)
-    factor = jnp.maximum(0.0, 1.0 - DUAL_STEP * radius / jnp.sqrt(total + NORM_EPS))
-    factor_ref[...] = jnp.broadcast_to(factor, (1, COLS))
 
     for at, copy in enumerate(halos):
         if at % 3 == 0:
@@ -442,8 +440,34 @@
 
     pl.when(is_early)(early_sent)
     pl.when(is_late)(lambda: sent(line_in, EARLY, line_sem.at[0]))
+
+    pl.when(is_early)(finish)
+    pl.when(is_late)(lambda: total_copy(0).wait_recv())
+    total = jnp.sum(total_in[...], axis=1, keepdims=True)
+    radius = BALL_SCALE * math.sqrt(CHANNELS * ROWS * COLS * fy_count * fx_count)
+    factor = jnp.maximum(0.0, 1.0 - DUAL_STEP * radius / jnp.sqrt(total + NORM_EPS))
+    factor_ref[...] = jnp.broadcast_to(factor, (1, COLS))
+
+    for z, zs in shares.items():
+        pl.when(me_x == z)(functools.partial(hand, zs))
     for z, zs in shares.items():
         pl.when(me_x == z)(functools.partial(sent, line_in, len(zs), total_sem.at[0]))
+
+
+def last_step(pa_ref, pb_ref, shifted_ref, factor_ref, image_hbm, dual_hbm, image, dual, sems):
+    factor = factor_ref[...]
+    copies = []
+    for part in range(4):
+        for c in range(4 * part, 4 * part + 4):
+            image[c] = jnp.maximum(pa_ref[c] - factor * pb_ref[c], 0.0)
+            dual[c] = factor * shifted_ref[c]
+        chans = pl.ds(4 * part, 4)
+        for at, (source, target) in enumerate([(image, image_hbm), (dual, dual_hbm)]):
+            copy = pltpu.make_async_copy(source.at[chans], target.at[chans], sems.at[part, at])
+            copy.start()
+            copies.append(copy)
+    for copy in copies:
+        copy.wait()
 
 
 def per_device(fy_count, fx_count, start_image, dirty, sampling, basis_seed, margin):
@@ -478,15 +502,22 @@
             pltpu.VMEM((1, COLS), F32), pltpu.VMEM((fx_count, 1, COLS), F32),
             pltpu.VMEM((1, COLS), F32), pltpu.VMEM((fy_count, 1, COLS), F32),
             pltpu.VMEM((1, COLS), F32), pltpu.VMEM((1, COLS), F32),
-            dma((8,)), dma((HALVES, 3)), dma((HALVES, 3)), dma((2,)), dma((2,)), dma((2,)), dma((HALVES, 3)), dma((HALVES, 3)),
+            dma((4, 3)), dma((5,)), dma((HALVES, 3)), dma((HALVES, 3)), dma((2,)), dma((2,)), dma((2,)), dma((HALVES, 3)), dma((HALVES, 3)),
         ],
         compiler_params=pltpu.CompilerParams(collective_id=0, has_side_effects=True, vmem_limit_bytes=40 * 1024 * 1024),
         name="step",
     )(*(pltpu.with_memory_space_constraint(value, pltpu.HBM) for value in (
         start_image, dirty, sampling, basis_seed.T, margin,
         jnp.asarray(forward, F32), jnp.asarray(backward, F32), jnp.asarray(column, BF))))
-    factor = factor[0, 0]
-    return jnp.maximum(pa - factor * pb, 0.0), factor * shifted
+    return pl.pallas_call(
+        last_step,
+        out_shape=(tile, tile),
+        in_specs=[vmem] * 4,
+        out_specs=(hbm, hbm),
+        scratch_shapes=[field, field, dma((4, 2))],
+        compiler_params=pltpu.CompilerParams(vmem_limit_bytes=4 * 1024 * 1024),
+        name="last",
+    )(pa, pb, shifted, factor)
 
 
 def solution(mesh):

time: 28.2 us -> 27.5 us (0.975)
  other arithmetic: 0.89 us -> 0 us
    max x1 -> x0, other arithmetic: 0.89 us -> none  [per_device(): return (jnp.maximum(pa - factor * pb, 0.0), factor * shifted)]
    pallas_call x0 -> x1, Pallas kernels: none -> 0.86 us  [per_device(): pl.pallas_call(last_step, out_shape=(tile, tile), in_specs=[vmem] * 4, ou...]
    pallas_call x1, Pallas kernels: 26.5 us -> 25.8 us  [per_device(): pl.pallas_call(body, out_shape=(tile, tile, tile, jax.ShapeDtypeStruct((1...]
where the time goes in v4:
time: 27.5 us; the launch traced here: 27.3 us
  Pallas kernels  26.7 us (97%)
  between operations  0.64 us (2%)
    pallas_call x1, Pallas kernels, per_device(): pl.pallas_call(body, out_shape=(tile, tile, tile, jax.ShapeDtypeStruct((1...  25.8 us
    pallas_call x1, Pallas kernels, per_device(): pl.pallas_call(last_step, out_shape=(tile, tile), in_specs=[vmem] * 4, ou...  0.86 us

profile of v4, /device:TPU:1, one launch (start us, length us, event | category | flops | bytes accessed | tf_op | source)
XLA Modules:
  0.0 27.3 jit_solution(7965948681225540987)
XLA Ops:
  0.6 25.8 %step.1 = (f32[16,32,128]{2,1,0:T(8,128)S(1)}, f32[16,32,128]{2,1,0:T(8,128)S(1)}, f32[16,32,128]{2,1,0:T(8,128)S(1)}, f32[1,128]{1,0:T(1,128)S(1)}) custom-call(f32[16,32,128]{2,1,0:T(8,128)} %refs_0_.1, f32[16,32,128]{2,1,0:T(8,128)} %refs_1_.1, f32[16,32,128]{2,1,0:T(8,128)} %refs_2_.1, f32[4,16]{1,0:T(4,128)} %bitcast.1, s32[1,1,2,2]{3,2,1,0:T(2,128)} %refs_4_.1, ...), custom_call_target="tpu_custom_call" | custom-call | tf_op jit(solution)/shard_map/step/pallas_call | solution.py:485
  26.5 0.9 %last.1 = (f32[16,32,128]{2,1,0:T(8,128)}, f32[16,32,128]{2,1,0:T(8,128)}) custom-call(f32[16,32,128]{2,1,0:T(8,128)S(1)} %get-tuple-element.6.pa_ref, f32[16,32,128]{2,1,0:T(8,128)S(1)} %get-tuple-element.7.pb_ref, f32[16,32,128]{2,1,0:T(8,128)S(1)} %get-tuple-element.8.shifted_ref, f32[1,128]{1,0:T(1,128)S(1)} %get-tuple-element.9.factor_ref), custom_call_target="tpu_custom_call" | custom-call | tf_op jit(solution)/shard_map/last/pallas_call | solution.py:512

commit v5 on v4

--- a/solution.py
+++ b/solution.py
@@ -21,6 +21,8 @@
 RANK = 4
 HALVES = 2
 EARLY = 4
+FIRST = 1
+FAR = 4
 PER = CHANNELS // HALVES
 GROUPS = CHANNELS // 4
 
@@ -106,8 +108,8 @@
                 start, dirty, samp, basis, margin, fwd_raw, bwd_raw, col,
                 fwd_m, bwd_m, pack, above, left_in, corner_in,
                 x_own, x_left, lhs, bands, z_own, z_left, own, up_out, left_out, up_in, left_back, corner_back,
-                spec, line_out, line_in, plane_out, plane_in, total_out, total_in,
-                input_sem, load_sem, halo_send, halo_recv, line_sem, plane_sem, total_sem, back_send, back_recv):
+                spec, line_out, line_in, plane_out, plane_in, side_out, direct_in, total_out, total_in,
+                input_sem, load_sem, halo_send, halo_recv, line_sem, plane_sem, direct_sem, total_sem, back_send, back_recv):
     me_y, me_x = lax.axis_index("fy"), lax.axis_index("fx")
     below, over = lax.rem(me_y + 1, fy_count), lax.rem(me_y + fy_count - 1, fy_count)
     right, left = lax.rem(me_x + 1, fx_count), lax.rem(me_x + fx_count - 1, fx_count)
@@ -145,6 +147,18 @@
     is_early, is_late = me_x < EARLY, me_x >= EARLY
     has_left, has_right = me_x > 0, me_x < fx_count - 1
 
+    far0 = fx_count // 2 - 1
+    is_far = jnp.logical_and(me_x >= far0, me_x < far0 + FAR)
+    is_first = jnp.logical_and(me_x == 0, me_y == FIRST)
+
+    def greet_far():
+        for z in range(far0, far0 + FAR):
+            def each(k, carry, z=z):
+                greet({"fy": lax.rem(me_y + k, fy_count), "fx": z})
+                return carry
+
+            lax.fori_loop(1, fy_count, each, 0)
+
     def greet_many():
         for k in order:
             greet(line[k])
@@ -157,6 +171,7 @@
         greet({"fy": me_y, "fx": left})
 
     pl.when(is_early)(greet_many)
+    pl.when(is_first)(greet_far)
     pl.when(is_late)(greet_few)
     pl.when(jnp.logical_and(is_late, has_right))(lambda: greet({"fy": me_y, "fx": right}))
     pl.when(has_right)(lambda: greet({"fy": below, "fx": right}))
@@ -180,14 +195,18 @@
     guests = jnp.where(
         is_early,
         len(plane) + EARLY - 1 + one(me_x == EARLY - 1) + one(has_left) + 1,
-        2 + EARLY + one(me_x > EARLY) + 1 + 2 * one(has_right))
+        2 + EARLY + one(me_x > EARLY) + 1 + 2 * one(has_right) + one(jnp.logical_and(is_far, me_y != FIRST)))
     pl.semaphore_wait(barrier, guests)
 
     def line_copy(z):
         return pltpu.make_async_remote_copy(
-            src_ref=line_out, dst_ref=line_in.at[me_x], send_sem=line_sem.at[0], recv_sem=line_sem.at[1],
+            src_ref=line_out, dst_ref=line_in.at[me_x], send_sem=line_sem.at[0], recv_sem=line_sem.at[1 + one(is_far)],
             device_id={"fy": me_y, "fx": z}, device_id_type=MESH)
 
+    direct = pltpu.make_async_remote_copy(
+        src_ref=line_out, dst_ref=direct_in.at[lax.rem(me_x, FAR) * fy_count + me_y], send_sem=direct_sem.at[0],
+        recv_sem=direct_sem.at[1], device_id={"fy": FIRST, "fx": 0}, device_id_type=MESH)
+    pl.when(is_far)(direct.start)
     for z in range(EARLY):
         pl.when(me_x != z)(lambda z=z: line_copy(z).start())
 
@@ -374,16 +393,31 @@
                 pl.when(has_left)(copy.start)
             backs.append(copy)
 
+    def arrived(ref, count, sem):
+        pltpu.make_async_copy(ref.at[pl.ds(0, count)], ref.at[pl.ds(0, count)], sem).wait()
+
+    def plane_copy(source, device):
+        return pltpu.make_async_remote_copy(
+            src_ref=source, dst_ref=plane_in.at[me_y], send_sem=plane_sem.at[0], recv_sem=plane_sem.at[1],
+            device_id=device, device_id_type=MESH)
+
     def exchange():
-        pltpu.make_async_copy(line_in.at[pl.ds(0, fx_count - 1)], line_in.at[pl.ds(0, fx_count - 1)], line_sem.at[1]).wait()
+        arrived(line_in, fx_count - 1 - FAR, line_sem.at[1])
         line_in[me_x] = line_out[...]
-        partial = jnp.sum(line_in[...], axis=0)
-        plane_out[...] = partial
-        plane_in[me_y] = partial
+        side = jnp.sum(line_in[0:far0], axis=0) + jnp.sum(line_in[far0 + FAR :], axis=0)
+        side_out[...] = side
+        plane_in[me_y] = side
+        pl.when(jnp.logical_and(me_x == 0, me_y != FIRST))(plane_copy(side_out, {"fy": FIRST, "fx": 0}).start)
+        arrived(line_in, FAR, line_sem.at[2])
+        whole = side_out[...] + jnp.sum(line_in[far0 : far0 + FAR], axis=0)
+        plane_out[...] = whole
+
+        def keep_whole():
+            plane_in[me_y] = whole
+
+        pl.when(jnp.logical_not(is_first))(keep_whole)
         for device in plane:
-            pltpu.make_async_remote_copy(
-                src_ref=plane_out, dst_ref=plane_in.at[me_y], send_sem=plane_sem.at[0], recv_sem=plane_sem.at[1],
-                device_id=device, device_id_type=MESH).start()
+            pl.when(jnp.logical_or(me_x != 0, device["fy"] != FIRST))(plane_copy(plane_out, device).start)
 
     pl.when(is_early)(exchange)
 
@@ -407,14 +441,17 @@
             src_ref=total_out, dst_ref=total_in, send_sem=total_sem.at[0], recv_sem=total_sem.at[1],
             device_id={"fy": me_y, "fx": z}, device_id_type=MESH)
 
-    middle = (EARLY - 1 + fx_count) // 2 + 1
-    shares = {EARLY - 2: range(fx_count - 1, middle, -1), EARLY - 1: range(EARLY, middle + 1)}
+    shares = {EARLY - 1: sorted(range(EARLY, fx_count), key=lambda z: abs(z - EARLY + 1 - fx_count // 2))}
 
     def finish():
-        pltpu.make_async_copy(plane_in.at[pl.ds(0, fy_count - 1)], plane_in.at[pl.ds(0, fy_count - 1)], plane_sem.at[1]).wait()
+        arrived(plane_in, fy_count - 1, plane_sem.at[1])
         total = jnp.sum(plane_in[...], axis=0)
         total_in[...] = total
         total_out[...] = total
+
+    def add_far():
+        arrived(direct_in, FAR * fy_count, direct_sem.at[1])
+        total_in[...] = total_in[...] + jnp.sum(direct_in[...], axis=0)
 
     def hand(zs):
         for z in zs:
@@ -431,17 +468,16 @@
         else:
             pl.when(has_left)(copy.wait_send)
 
-    def sent(ref, count, sem):
-        pltpu.make_async_copy(ref.at[pl.ds(0, count)], ref.at[pl.ds(0, count)], sem).wait()
-
     def early_sent():
-        sent(line_in, EARLY - 1, line_sem.at[0])
-        sent(plane_in, fy_count - 1, plane_sem.at[0])
+        arrived(line_in, EARLY - 1, line_sem.at[0])
+        arrived(plane_in, fy_count - 1, plane_sem.at[0])
 
     pl.when(is_early)(early_sent)
-    pl.when(is_late)(lambda: sent(line_in, EARLY, line_sem.at[0]))
+    pl.when(is_late)(lambda: arrived(line_in, EARLY, line_sem.at[0]))
+    pl.when(is_far)(direct.wait_send)
 
     pl.when(is_early)(finish)
+    pl.when(is_first)(add_far)
     pl.when(is_late)(lambda: total_copy(0).wait_recv())
     total = jnp.sum(total_in[...], axis=1, keepdims=True)
     radius = BALL_SCALE * math.sqrt(CHANNELS * ROWS * COLS * fy_count * fx_count)
@@ -451,7 +487,7 @@
     for z, zs in shares.items():
         pl.when(me_x == z)(functools.partial(hand, zs))
     for z, zs in shares.items():
-        pl.when(me_x == z)(functools.partial(sent, line_in, len(zs), total_sem.at[0]))
+        pl.when(me_x == z)(functools.partial(arrived, line_in, len(zs), total_sem.at[0]))
 
 
 def last_step(pa_ref, pb_ref, shifted_ref, factor_ref, image_hbm, dual_hbm, image, dual, sems):
@@ -501,8 +537,9 @@
             pltpu.VMEM((RANK, CHANNELS, COLS), F32),
             pltpu.VMEM((1, COLS), F32), pltpu.VMEM((fx_count, 1, COLS), F32),
             pltpu.VMEM((1, COLS), F32), pltpu.VMEM((fy_count, 1, COLS), F32),
+            pltpu.VMEM((1, COLS), F32), pltpu.VMEM((FAR * fy_count, 1, COLS), F32),
             pltpu.VMEM((1, COLS), F32), pltpu.VMEM((1, COLS), F32),
-            dma((4, 3)), dma((5,)), dma((HALVES, 3)), dma((HALVES, 3)), dma((2,)), dma((2,)), dma((2,)), dma((HALVES, 3)), dma((HALVES, 3)),
+            dma((4, 3)), dma((5,)), dma((HALVES, 3)), dma((HALVES, 3)), dma((3,)), dma((2,)), dma((2,)), dma((2,)), dma((HALVES, 3)), dma((HALVES, 3)),
         ],
         compiler_params=pltpu.CompilerParams(collective_id=0, has_side_effects=True, vmem_limit_bytes=40 * 1024 * 1024),
         name="step",

time: 27.5 us -> 26.4 us (0.960)
  Pallas kernels: 26.7 us -> 25.5 us
    pallas_call x1, Pallas kernels: 25.8 us -> 24.6 us  [per_device(): pl.pallas_call(body, out_shape=(tile, tile, tile, jax.ShapeDtypeStruct((1...]
where the time goes in v5:
time: 26.4 us; the launch traced here: 26.1 us
  Pallas kernels  25.5 us (97%)
  between operations  0.64 us (2%)
    pallas_call x1, Pallas kernels, per_device(): pl.pallas_call(body, out_shape=(tile, tile, tile, jax.ShapeDtypeStruct((1...  24.6 us
    pallas_call x1, Pallas kernels, per_device(): pl.pallas_call(last_step, out_shape=(tile, tile), in_specs=[vmem] * 4, ou...  0.86 us

profile of v5, /device:TPU:1, one launch (start us, length us, event | category | flops | bytes accessed | tf_op | source)
XLA Modules:
  0.0 26.1 jit_solution(564282852456455916)
XLA Ops:
  0.6 24.6 %step.1 = (f32[16,32,128]{2,1,0:T(8,128)S(1)}, f32[16,32,128]{2,1,0:T(8,128)S(1)}, f32[16,32,128]{2,1,0:T(8,128)S(1)}, f32[1,128]{1,0:T(1,128)S(1)}) custom-call(f32[16,32,128]{2,1,0:T(8,128)} %refs_0_.1, f32[16,32,128]{2,1,0:T(8,128)} %refs_1_.1, f32[16,32,128]{2,1,0:T(8,128)} %refs_2_.1, f32[4,16]{1,0:T(4,128)} %bitcast.1, s32[1,1,2,2]{3,2,1,0:T(2,128)} %refs_4_.1, ...), custom_call_target="tpu_custom_call" | custom-call | tf_op jit(solution)/shard_map/step/pallas_call | solution.py:521
  25.3 0.9 %last.1 = (f32[16,32,128]{2,1,0:T(8,128)}, f32[16,32,128]{2,1,0:T(8,128)}) custom-call(f32[16,32,128]{2,1,0:T(8,128)S(1)} %get-tuple-element.6.pa_ref, f32[16,32,128]{2,1,0:T(8,128)S(1)} %get-tuple-element.7.pb_ref, f32[16,32,128]{2,1,0:T(8,128)S(1)} %get-tuple-element.8.shifted_ref, f32[1,128]{1,0:T(1,128)S(1)} %get-tuple-element.9.factor_ref), custom_call_target="tpu_custom_call" | custom-call | tf_op jit(solution)/shard_map/last/pallas_call | solution.py:549

commit v6 on v5

--- a/solution.py
+++ b/solution.py
@@ -22,7 +22,7 @@
 HALVES = 2
 EARLY = 4
 FIRST = 1
-FAR = 4
+FAR = 6
 PER = CHANNELS // HALVES
 GROUPS = CHANNELS // 4
 
@@ -88,9 +88,9 @@
     backward = np.concatenate([hi.T, hi.T, lo.T], axis=1)
     column = []
     for level in range(LEVELS):
-        column.append(split_host(cols[level])[0])
+        column.extend(split_host(cols[level]))
     for level in range(LEVELS):
-        column.append(split_host(cols[level].T)[0])
+        column.extend(split_host(cols[level].T))
     return forward, backward, np.stack(column)
 
 
@@ -147,7 +147,7 @@
     is_early, is_late = me_x < EARLY, me_x >= EARLY
     has_left, has_right = me_x > 0, me_x < fx_count - 1
 
-    far0 = fx_count // 2 - 1
+    far0 = fx_count // 2 - 2
     is_far = jnp.logical_and(me_x >= far0, me_x < far0 + FAR)
     is_first = jnp.logical_and(me_x == 0, me_y == FIRST)
 
@@ -345,7 +345,7 @@
                     lhs[l, pl.ds(64 * c, 64), 384:512] = low
         z_sum = [[jnp.zeros((64, COLS), F32) for l in range(LEVELS)] for g in range(PER // 4)]
         for l in range(LEVELS):
-            acc = dot(lhs[l, :, 0:256], col[l]) + dot(lhs[l, :, 256:512], col[l])
+            acc = dot(lhs[l, :, 0:256], col[2 * l]) + dot(lhs[l, :, 256:512], col[2 * l]) + dot(lhs[l, :, 0:256], col[2 * l + 1])
             acc = jnp.clip(acc, -CLIP_LEVEL, CLIP_LEVEL)
             high, low = split(acc)
             for c in range(PER):
@@ -357,7 +357,8 @@
                 bands[pl.ds(top, 32), 384:512] = low[top:mid, 128:256]
                 bands[pl.ds(mid, 32), 0:256] = high[mid:end, :]
                 bands[pl.ds(mid, 32), 256:512] = low[mid:end, :]
-            z = dot(bands[:, 0:256], col[LEVELS + l]) + dot(bands[:, 256:512], col[LEVELS + l])
+            at = 2 * LEVELS + 2 * l
+            z = dot(bands[:, 0:256], col[at]) + dot(bands[:, 256:512], col[at]) + dot(bands[:, 0:256], col[at + 1])
             for c in range(PER):
                 high, low = split(z[64 * c : 64 * c + 64, 0:128])
                 lanes = pl.ds(COLS * (c % 2), COLS)
@@ -527,7 +528,7 @@
             field, field, field,
             pltpu.VMEM((RANK, CHANNELS), F32),
             pltpu.SMEM((1, 1, LEVELS, 2), jnp.int32),
-            pltpu.VMEM((128, 192), F32), pltpu.VMEM((64, 384), F32), pltpu.VMEM((2 * LEVELS, 256, 256), BF),
+            pltpu.VMEM((128, 192), F32), pltpu.VMEM((64, 384), F32), pltpu.VMEM((4 * LEVELS, 256, 256), BF),
             pltpu.VMEM((128, 192), BF), pltpu.VMEM((64, 384), BF),
             strips, field, strips, strips,
             pltpu.VMEM((CHANNELS // 2, 192, 256), BF), pltpu.VMEM((GROUPS, 192, COLS), BF),

time: 26.4 us -> 25.9 us (0.981)
  Pallas kernels: 25.5 us -> 25.1 us
    pallas_call x1, Pallas kernels: 24.6 us -> 24.2 us  [per_device(): pl.pallas_call(body, out_shape=(tile, tile, tile, jax.ShapeDtypeStruct((1...]
where the time goes in v6:
time: 25.9 us; the launch traced here: 25.7 us
  Pallas kernels  25.1 us (97%)
  between operations  0.64 us (2%)
    pallas_call x1, Pallas kernels, per_device(): pl.pallas_call(body, out_shape=(tile, tile, tile, jax.ShapeDtypeStruct((1...  24.2 us
    pallas_call x1, Pallas kernels, per_device(): pl.pallas_call(last_step, out_shape=(tile, tile), in_specs=[vmem] * 4, ou...  0.86 us

profile of v6, /device:TPU:1, one launch (start us, length us, event | category | flops | bytes accessed | tf_op | source)
XLA Modules:
  0.0 25.7 jit_solution(2312781243642231596)
XLA Ops:
  0.6 24.2 %step.1 = (f32[16,32,128]{2,1,0:T(8,128)S(1)}, f32[16,32,128]{2,1,0:T(8,128)S(1)}, f32[16,32,128]{2,1,0:T(8,128)S(1)}, f32[1,128]{1,0:T(1,128)S(1)}) custom-call(f32[16,32,128]{2,1,0:T(8,128)} %refs_0_.1, f32[16,32,128]{2,1,0:T(8,128)} %refs_1_.1, f32[16,32,128]{2,1,0:T(8,128)} %refs_2_.1, f32[4,16]{1,0:T(4,128)} %bitcast.1, s32[1,1,2,2]{3,2,1,0:T(2,128)} %refs_4_.1, ...), custom_call_target="tpu_custom_call" | custom-call | tf_op jit(solution)/shard_map/step/pallas_call | solution.py:522
  24.9 0.9 %last.1 = (f32[16,32,128]{2,1,0:T(8,128)}, f32[16,32,128]{2,1,0:T(8,128)}) custom-call(f32[16,32,128]{2,1,0:T(8,128)S(1)} %get-tuple-element.6.pa_ref, f32[16,32,128]{2,1,0:T(8,128)S(1)} %get-tuple-element.7.pb_ref, f32[16,32,128]{2,1,0:T(8,128)S(1)} %get-tuple-element.8.shifted_ref, f32[1,128]{1,0:T(1,128)S(1)} %get-tuple-element.9.factor_ref), custom_call_target="tpu_custom_call" | custom-call | tf_op jit(solution)/shard_map/last/pallas_call | solution.py:550

commit v7 on v6

--- a/solution.py
+++ b/solution.py
@@ -20,8 +20,8 @@
 CHANNELS = 16
 RANK = 4
 HALVES = 2
-EARLY = 4
-FIRST = 1
+EARLY = 5
+FIRSTS = ((0, 1), (0, 3), (0, 9), (0, 2), (0, 8), (1, 1), (1, 0))
 FAR = 6
 PER = CHANNELS // HALVES
 GROUPS = CHANNELS // 4
@@ -146,10 +146,12 @@
     order = sorted(line, key=lambda k: -min(k, fx_count - k))
     is_early, is_late = me_x < EARLY, me_x >= EARLY
     has_left, has_right = me_x > 0, me_x < fx_count - 1
+    has_above, has_below = me_y > 0, me_y < fy_count - 1
+    up_left, down_right = jnp.logical_and(has_above, has_left), jnp.logical_and(has_below, has_right)
 
     far0 = fx_count // 2 - 2
     is_far = jnp.logical_and(me_x >= far0, me_x < far0 + FAR)
-    is_first = jnp.logical_and(me_x == 0, me_y == FIRST)
+    is_first = functools.reduce(jnp.logical_or, [jnp.logical_and(me_x == z, me_y == y) for z, y in FIRSTS])
 
     def greet_far():
         for z in range(far0, far0 + FAR):
@@ -166,16 +168,16 @@
             greet(device)
 
     def greet_few():
-        greet({"fy": over, "fx": me_x})
-        greet({"fy": below, "fx": me_x})
+        pl.when(has_above)(lambda: greet({"fy": over, "fx": me_x}))
+        pl.when(has_below)(lambda: greet({"fy": below, "fx": me_x}))
         greet({"fy": me_y, "fx": left})
 
     pl.when(is_early)(greet_many)
     pl.when(is_first)(greet_far)
     pl.when(is_late)(greet_few)
     pl.when(jnp.logical_and(is_late, has_right))(lambda: greet({"fy": me_y, "fx": right}))
-    pl.when(has_right)(lambda: greet({"fy": below, "fx": right}))
-    pl.when(has_left)(lambda: greet({"fy": over, "fx": left}))
+    pl.when(down_right)(lambda: greet({"fy": below, "fx": right}))
+    pl.when(up_left)(lambda: greet({"fy": over, "fx": left}))
 
     lane = lax.broadcasted_iota(jnp.int32, (1, COLS), 1)
     block = lane // PAD
@@ -194,8 +196,9 @@
     one = lambda flag: flag.astype(jnp.int32)
     guests = jnp.where(
         is_early,
-        len(plane) + EARLY - 1 + one(me_x == EARLY - 1) + one(has_left) + 1,
-        2 + EARLY + one(me_x > EARLY) + 1 + 2 * one(has_right) + one(jnp.logical_and(is_far, me_y != FIRST)))
+        len(plane) + EARLY - 1 + one(me_x == EARLY - 1),
+        one(has_above) + one(has_below) + EARLY + one(me_x > EARLY) + one(has_right)
+        + one(is_far) * sum(one(me_y != y) for z, y in FIRSTS)) + one(up_left) + one(down_right)
     pl.semaphore_wait(barrier, guests)
 
     def line_copy(z):
@@ -203,10 +206,17 @@
             src_ref=line_out, dst_ref=line_in.at[me_x], send_sem=line_sem.at[0], recv_sem=line_sem.at[1 + one(is_far)],
             device_id={"fy": me_y, "fx": z}, device_id_type=MESH)
 
-    direct = pltpu.make_async_remote_copy(
-        src_ref=line_out, dst_ref=direct_in.at[lax.rem(me_x, FAR) * fy_count + me_y], send_sem=direct_sem.at[0],
-        recv_sem=direct_sem.at[1], device_id={"fy": FIRST, "fx": 0}, device_id_type=MESH)
-    pl.when(is_far)(direct.start)
+    directs = []
+    for z, y in FIRSTS:
+        directs.append(pltpu.make_async_remote_copy(
+            src_ref=line_out, dst_ref=direct_in.at[lax.rem(me_x, FAR) * fy_count + me_y], send_sem=direct_sem.at[0],
+            recv_sem=direct_sem.at[1 + lax.rem(me_x, FAR)], device_id={"fy": y, "fx": z}, device_id_type=MESH))
+
+    def send_direct():
+        for copy in directs:
+            copy.start()
+
+    pl.when(is_far)(send_direct)
     for z in range(EARLY):
         pl.when(me_x != z)(lambda z=z: line_copy(z).start())
 
@@ -232,22 +242,19 @@
             copy = pltpu.make_async_remote_copy(
                 src_ref=source, dst_ref=target, send_sem=halo_send.at[h, at], recv_sem=halo_recv.at[h, at],
                 device_id=device, device_id_type=MESH)
-            if at == 0:
-                copy.start()
-            else:
-                pl.when(has_right)(copy.start)
+            pl.when((has_below, has_right, down_right)[at])(copy.start)
             halos.append(copy)
 
-    def no_left():
-        left_in[...] = jnp.zeros_like(left_in)
-        corner_in[...] = jnp.zeros_like(corner_in)
-
-    def no_right():
-        left_back[...] = jnp.zeros_like(left_back)
-        corner_back[...] = jnp.zeros_like(corner_back)
-
-    pl.when(jnp.logical_not(has_left))(no_left)
-    pl.when(jnp.logical_not(has_right))(no_right)
+    def clear(*refs):
+        for ref in refs:
+            ref[...] = jnp.zeros_like(ref)
+
+    pl.when(jnp.logical_not(has_above))(functools.partial(clear, above))
+    pl.when(jnp.logical_not(has_left))(functools.partial(clear, left_in))
+    pl.when(jnp.logical_not(up_left))(functools.partial(clear, corner_in))
+    pl.when(jnp.logical_not(has_below))(functools.partial(clear, up_in))
+    pl.when(jnp.logical_not(has_right))(functools.partial(clear, left_back))
+    pl.when(jnp.logical_not(down_right))(functools.partial(clear, corner_back))
 
     for copy in loads:
         copy.wait()
@@ -313,13 +320,8 @@
 
     backs = []
     for h in range(HALVES):
-        halos[3 * h].wait_recv()
-
-        def from_left(h=h):
-            halos[3 * h + 1].wait_recv()
-            halos[3 * h + 2].wait_recv()
-
-        pl.when(has_left)(from_left)
+        for flag, copy in zip((has_above, has_left, up_left), halos[3 * h : 3 * h + 3]):
+            pl.when(flag)(copy.wait_recv)
         first = h * PER
         for c in range(first, first + PER):
             place(x_own, c // 2, c % 2, 0, above[c])
@@ -388,10 +390,7 @@
             copy = pltpu.make_async_remote_copy(
                 src_ref=source, dst_ref=target, send_sem=back_send.at[h, at], recv_sem=back_recv.at[h, at],
                 device_id=device, device_id_type=MESH)
-            if at == 2:
-                copy.start()
-            else:
-                pl.when(has_left)(copy.start)
+            pl.when((has_left, up_left, has_above)[at])(copy.start)
             backs.append(copy)
 
     def arrived(ref, count, sem):
@@ -408,7 +407,8 @@
         side = jnp.sum(line_in[0:far0], axis=0) + jnp.sum(line_in[far0 + FAR :], axis=0)
         side_out[...] = side
         plane_in[me_y] = side
-        pl.when(jnp.logical_and(me_x == 0, me_y != FIRST))(plane_copy(side_out, {"fy": FIRST, "fx": 0}).start)
+        for z, y in FIRSTS:
+            pl.when(jnp.logical_and(me_x == z, me_y != y))(plane_copy(side_out, {"fy": y, "fx": z}).start)
         arrived(line_in, FAR, line_sem.at[2])
         whole = side_out[...] + jnp.sum(line_in[far0 : far0 + FAR], axis=0)
         plane_out[...] = whole
@@ -417,16 +417,21 @@
             plane_in[me_y] = whole
 
         pl.when(jnp.logical_not(is_first))(keep_whole)
-        for device in plane:
-            pl.when(jnp.logical_or(me_x != 0, device["fy"] != FIRST))(plane_copy(plane_out, device).start)
+
+        def send_whole(skip):
+            for y in sorted(range(fy_count), key=lambda y: min(y // 8, 4 - y // 8) + min(y // 2 % 4, 4 - y // 2 % 4)):
+                if y not in skip:
+                    pl.when(me_y != y)(plane_copy(plane_out, {"fy": y, "fx": me_x}).start)
+
+        special = sorted({z for z, y in FIRSTS})
+        for at in special:
+            pl.when(me_x == at)(functools.partial(send_whole, [y for z, y in FIRSTS if z == at]))
+        pl.when(me_x > special[-1])(functools.partial(send_whole, []))
 
     pl.when(is_early)(exchange)
 
     for at, copy in enumerate(backs):
-        if at % 3 == 2:
-            copy.wait_recv()
-        else:
-            pl.when(has_right)(copy.wait_recv)
+        pl.when((has_right, down_right, has_below)[at % 3])(copy.wait_recv)
     for g in range(GROUPS):
         strip = left_back[g] + corner_back[g]
         for q in range(4):
@@ -442,7 +447,8 @@
             src_ref=total_out, dst_ref=total_in, send_sem=total_sem.at[0], recv_sem=total_sem.at[1],
             device_id={"fy": me_y, "fx": z}, device_id_type=MESH)
 
-    shares = {EARLY - 1: sorted(range(EARLY, fx_count), key=lambda z: abs(z - EARLY + 1 - fx_count // 2))}
+    middle = (2 * EARLY + fx_count - 5) // 2
+    shares = {EARLY - 2: range(middle + 1, fx_count), EARLY - 1: range(middle, EARLY - 1, -1)}
 
     def finish():
         arrived(plane_in, fy_count - 1, plane_sem.at[1])
@@ -451,23 +457,21 @@
         total_out[...] = total
 
     def add_far():
-        arrived(direct_in, FAR * fy_count, direct_sem.at[1])
-        total_in[...] = total_in[...] + jnp.sum(direct_in[...], axis=0)
+        total = total_in[...]
+        for z in sorted(range(far0, far0 + FAR), key=lambda z: -abs(z - far0 - 2.4)):
+            at = z % FAR
+            arrived(direct_in, fy_count, direct_sem.at[1 + at])
+            total = total + jnp.sum(direct_in[at * fy_count : (at + 1) * fy_count], axis=0)
+        total_in[...] = total
 
     def hand(zs):
         for z in zs:
             total_copy(z).start()
 
     for at, copy in enumerate(halos):
-        if at % 3 == 0:
-            copy.wait_send()
-        else:
-            pl.when(has_right)(copy.wait_send)
+        pl.when((has_below, has_right, down_right)[at % 3])(copy.wait_send)
     for at, copy in enumerate(backs):
-        if at % 3 == 2:
-            copy.wait_send()
-        else:
-            pl.when(has_left)(copy.wait_send)
+        pl.when((has_left, up_left, has_above)[at % 3])(copy.wait_send)
 
     def early_sent():
         arrived(line_in, EARLY - 1, line_sem.at[0])
@@ -475,7 +479,7 @@
 
     pl.when(is_early)(early_sent)
     pl.when(is_late)(lambda: arrived(line_in, EARLY, line_sem.at[0]))
-    pl.when(is_far)(direct.wait_send)
+    pl.when(is_far)(lambda: arrived(line_in, len(FIRSTS), direct_sem.at[0]))
 
     pl.when(is_early)(finish)
     pl.when(is_first)(add_far)
@@ -540,7 +544,7 @@
             pltpu.VMEM((1, COLS), F32), pltpu.VMEM((fy_count, 1, COLS), F32),
             pltpu.VMEM((1, COLS), F32), pltpu.VMEM((FAR * fy_count, 1, COLS), F32),
             pltpu.VMEM((1, COLS), F32), pltpu.VMEM((1, COLS), F32),
-            dma((4, 3)), dma((5,)), dma((HALVES, 3)), dma((HALVES, 3)), dma((3,)), dma((2,)), dma((2,)), dma((2,)), dma((HALVES, 3)), dma((HALVES, 3)),
+            dma((4, 3)), dma((5,)), dma((HALVES, 3)), dma((HALVES, 3)), dma((3,)), dma((2,)), dma((1 + FAR,)), dma((2,)), dma((HALVES, 3)), dma((HALVES, 3)),
         ],
         compiler_params=pltpu.CompilerParams(collective_id=0, has_side_effects=True, vmem_limit_bytes=40 * 1024 * 1024),
         name="step",

time: 25.9 us -> 26 us (level)
  no operation moved by 1% of the time
where the time goes in v7:
time: 26 us; the launch traced here: 25.8 us
  Pallas kernels  25.2 us (97%)
  between operations  0.64 us (2%)
    pallas_call x1, Pallas kernels, per_device(): pl.pallas_call(body, out_shape=(tile, tile, tile, jax.ShapeDtypeStruct((1...  24.3 us
    pallas_call x1, Pallas kernels, per_device(): pl.pallas_call(last_step, out_shape=(tile, tile), in_specs=[vmem] * 4, ou...  0.86 us

profile of v7, /device:TPU:1, one launch (start us, length us, event | category | flops | bytes accessed | tf_op | source)
XLA Modules:
  0.0 25.8 jit_solution(16824978989837536262)
XLA Ops:
  0.6 24.3 %step.1 = (f32[16,32,128]{2,1,0:T(8,128)S(1)}, f32[16,32,128]{2,1,0:T(8,128)S(1)}, f32[16,32,128]{2,1,0:T(8,128)S(1)}, f32[1,128]{1,0:T(1,128)S(1)}) custom-call(f32[16,32,128]{2,1,0:T(8,128)} %refs_0_.1, f32[16,32,128]{2,1,0:T(8,128)} %refs_1_.1, f32[16,32,128]{2,1,0:T(8,128)} %refs_2_.1, f32[4,16]{1,0:T(4,128)} %bitcast.1, s32[1,1,2,2]{3,2,1,0:T(2,128)} %refs_4_.1, ...), custom_call_target="tpu_custom_call" | custom-call | tf_op jit(solution)/shard_map/step/pallas_call | solution.py:526
  25.0 0.9 %last.1 = (f32[16,32,128]{2,1,0:T(8,128)}, f32[16,32,128]{2,1,0:T(8,128)}) custom-call(f32[16,32,128]{2,1,0:T(8,128)S(1)} %get-tuple-element.6.pa_ref, f32[16,32,128]{2,1,0:T(8,128)S(1)} %get-tuple-element.7.pb_ref, f32[16,32,128]{2,1,0:T(8,128)S(1)} %get-tuple-element.8.shifted_ref, f32[1,128]{1,0:T(1,128)S(1)} %get-tuple-element.9.factor_ref), custom_call_target="tpu_custom_call" | custom-call | tf_op jit(solution)/shard_map/last/pallas_call | solution.py:554
